TPU v7x, 32 devices: a whole 2x2x4 slice. The times are simulated.
32 devices in a mesh: gx: 2 (over x), gy: 4 (over z), gz: 4 (over y, core).
Axes of the slice: x: 2, y: 2, z: 4, core: 2. Of those that a mesh axis runs over, the one named last changes fastest.
Arguments:
- inputs: bfloat16 [512, 6144], P(('gx', 'gz'), 'gy'), may hold values from -6 to 6
- norm_gain: float32 [6144], P('gy'), may hold values from 0.25 to 1.75
- norm_bias: float32 [6144], P('gy'), may hold values from -4 to 4
- pre_act: bfloat16 [512, 24576], P(('gx', 'gy'), 'gz'), may hold values from -8 to 8
- grad_act: bfloat16 [512, 24576], P(('gx', 'gy'), 'gz'), may hold values from -4 to 4
- up_weight: bfloat16 [4, 6144, 6144], P('gz', 'gx', 'gy'), may hold values from -0.078125 to 0.078125
Outputs:
- grad_inputs: bfloat16 [512, 6144], P(('gx', 'gz'), 'gy')
- grad_gain: float32 [6144], P('gy')
- grad_bias: float32 [6144], P('gy')
- grad_weight: float32 [4, 6144, 6144], P('gz', 'gx', 'gy')
All inputs are finite; a program needn't handle non-finite values.
Results may differ from a plain program's by a relative error of at most 0.0049.
Values may be sent and summed in bfloat16 or wider, within the bound.
A program may use at most 128 MiB of HBM per device.

v0:
```python
import jax
import jax.numpy as jnp
from jax import lax
from jax.sharding import PartitionSpec as P

D = 6144


epsilon = 1e-05
root_half = 0.7071067811865476
gauss_norm = 0.3989422804014327


def on_device(inputs, norm_gain, norm_bias, pre_act, grad_act, up_weight):
    widened = inputs.astype(jnp.float32)
    totals = lax.psum(jnp.sum(widened, axis=1), "gy")
    row_mean = totals / D
    centred = widened - row_mean[:, None]
    row_var = lax.psum(jnp.sum(centred * centred, axis=1), "gy") / D
    inv_std = lax.rsqrt(row_var + epsilon)[:, None]
    x_hat = centred * inv_std
    normed = (x_hat * norm_gain + norm_bias).astype(jnp.bfloat16)
    pre_float = pre_act.astype(jnp.float32)
    slopes = (
        0.5 * (1.0 + jax.scipy.special.erf(pre_float * root_half))
        + pre_float * jnp.exp(-0.5 * pre_float * pre_float) * gauss_norm
    )
    grad_local = (grad_act.astype(jnp.float32) * slopes).astype(jnp.bfloat16)
    grad_rows = lax.all_gather(grad_local, "gy", axis=0, tiled=True)
    partial_value = jnp.dot(
        grad_rows,
        lax.all_gather(up_weight, "gx", axis=1, tiled=True)[0],
        preferred_element_type=jnp.float32,
    )
    grad_normed = lax.psum_scatter(partial_value, "gz", scatter_dimension=0, tiled=True)
    normed_all = lax.all_gather(normed, ("gx", "gz"), axis=0, tiled=True)
    grad_cols = lax.all_to_all(grad_rows, "gx", split_axis=1, concat_axis=0, tiled=True)
    weight_block = lax.dot_general(
        grad_cols, normed_all, (((0,), (0,)), ((), ())), preferred_element_type=jnp.float32
    )
    grad_weight = weight_block.reshape(up_weight.shape)
    grad_gain, grad_bias = lax.psum(
        (jnp.sum(grad_normed * x_hat, axis=0), jnp.sum(grad_normed, axis=0)), ("gx", "gz")
    )
    scaled = grad_normed * norm_gain
    grad_sum, grad_dot = lax.psum((jnp.sum(scaled, axis=1), jnp.sum(scaled * x_hat, axis=1)), "gy")
    grad_inputs = inv_std * (scaled - grad_sum[:, None] / D - x_hat * (grad_dot[:, None] / D))
    return (grad_inputs.astype(jnp.bfloat16), grad_gain, grad_bias, grad_weight)


def solution(mesh):
    in_specs = (
        P(("gx", "gz"), "gy"),
        P("gy"),
        P("gy"),
        P(("gx", "gy"), "gz"),
        P(("gx", "gy"), "gz"),
        P("gz", "gx", "gy"),
    )
    out_specs = (P(("gx", "gz"), "gy"), P("gy"), P("gy"), P("gz", "gx", "gy"))
    return jax.shard_map(
        on_device, mesh=mesh, in_specs=in_specs, out_specs=out_specs, check_vma=False
    )
```

profile of v0, /device:TPU:0, one launch (start us, length us, event | category | flops | bytes accessed | tf_op | source)
XLA Modules:
  0.0 448.6 jit_solution(3603349197198858955)
XLA Ops:
  7.2 0.0 all-gather.4.cloned.1.call-start
  7.2 3.0 fusion.9
  10.2 0.0 all-gather.6.cloned.1.call-start
  10.3 0.7 all-gather.6.cloned.1.call-update
  11.0 0.0 reduce-scatter.2.cloned.1.call-start
  11.0 65.5 %all-gather.4.cloned.1.call-done = bf16[256,6144]{1,0:T(8,128)(2,1)} async-done(((bf16[64,6144]{1,0:T(8,128)(2,1)}), bf16[256,6144]{1,0:T(8,128)(2,1)}) %all-gather.4.cloned.1.call-update) | async-done | bytes 3145744 | tf_op jit(solution)/shard_map/all_gather | solution.py:29
  76.5 224.6 %all-gather.6.cloned.1.call-done = bf16[1,6144,1536]{2,1,0:T(8,128)(2,1)} async-done(((bf16[1,3072,1536]{2,1,0:T(8,128)(2,1)}), bf16[1,6144,1536]{2,1,0:T(8,128)(2,1)}) %all-gather.6.cloned.1.call-update) | async-done | bytes 18874384 | tf_op jit(solution)/shard_map/all_gather | solution.py:32
  301.1 10.7 %fusion = f32[256,1536]{1,0:T(8,128)} fusion(bf16[256,6144]{1,0:T(8,128)(2,1)} %all-gather.4.cloned.1.call-done, bf16[1,6144,1536]{2,1,0:T(8,128)(2,1)} %all-gather.6.cloned.1.call-done), kind=kOutput, calls=%fused_computation | convolution fusion | flops 4831838208 | bytes 23592960 | tf_op jit(solution)/shard_map/dot_general | solution.py:30
  311.9 0.0 all-gather.8.cloned.1.call-start
  311.9 0.8 copy-done
  312.8 0.1 convert_reduce_fusion
  312.9 11.7 %psum.42 = f32[64]{0:T(128)S(1)} all-reduce(f32[64]{0:T(128)S(1)} %convert_reduce_fusion), channel_id=1, replica_groups=mesh['gx'=2,'gy'=4,'gz'=4] {'gy'}, use_global_device_ids=true, to_apply=%region_1.0 | all-reduce | flops 64 | bytes 512 | tf_op jit(solution)/shard_map/psum | solution.py:16
  324.6 0.2 fusion.23
  324.8 8.4 %psum.43 = f32[64]{0:T(128)S(1)} all-reduce(f32[64]{0:T(128)S(1)} %fusion.23), channel_id=1, replica_groups=mesh['gx'=2,'gy'=4,'gz'=4] {'gy'}, use_global_device_ids=true, to_apply=%region_3.0 | all-reduce | flops 64 | bytes 512 | tf_op jit(solution)/shard_map/psum | solution.py:19
  333.2 6.9 %reduce-scatter.2.cloned.1.call-done = f32[64,1536]{1,0:T(8,128)} async-done(((f32[256,1536]{1,0:T(8,128)}), f32[64,1536]{1,0:T(8,128)}) %reduce-scatter.2.cloned.1.call-update) | async-done | bytes 393232 | tf_op jit(solution)/shard_map/reduce_scatter | solution.py:35
  340.1 2.0 fusion.20
  342.2 0.0 all-gather.8.cloned.1.call-update
  342.2 3.2 copy.13
  345.4 46.1 %all_to_all.19 = bf16[256,2,3072]{0,2,1:T(8,128)(2,1)} all-to-all(bf16[256,2,3072]{0,2,1:T(8,128)(2,1)S(1)} %bitcast.11), channel_id=1, replica_groups=mesh['gx'=2,'gy'=4,'gz'=4] {'gx'}, dimensions={1} | all-to-all | bytes 6291456 | tf_op jit(solution)/shard_map/all_to_all | solution.py:37
  391.5 3.2 copy.14
  394.6 11.7 %all-reduce.1 = (f32[64]{0:T(128)S(1)}, f32[64]{0:T(128)S(1)}) all-reduce(f32[64]{0:T(128)S(1)} %get-tuple-element.5, f32[64]{0:T(128)S(1)} %get-tuple-element.6), channel_id=1, replica_groups=mesh['gx'=2,'gy'=4,'gz'=4] {'gy'}, use_global_device_ids=true, to_apply=%region_8.0 | all-reduce | flops 128 | bytes 1024 | tf_op jit(solution)/shard_map/psum | solution.py:46
  406.3 22.9 %all-reduce = (f32[1536]{0:T(1024)}, f32[1536]{0:T(1024)}) all-reduce(f32[1536]{0:T(1024)S(1)} %get-tuple-element.4, f32[1536]{0:T(1024)S(1)} %get-tuple-element.7), channel_id=1, replica_groups=mesh['gx'=2,'gy'=4,'gz'=4] {'gx','gz'}, use_global_device_ids=true, to_apply=%region_10.0 | all-reduce | flops 3072 | bytes 24576 | tf_op jit(solution)/shard_map/psum | solution.py:42
  429.2 1.9 fusion.19
  431.1 10.9 %convolution_bitcast_fusion = f32[1,3072,1536]{2,1,0:T(8,128)} fusion(bf16[512,3072]{1,0:T(8,128)(2,1)S(1)} %bitcast.13, bf16[512,1536]{1,0:T(8,128)(2,1)} %all-gather.8.cloned.1.call-done), kind=kOutput, calls=%fused_computation.2 | convolution fusion | flops 4831838208 | bytes 23592960 | tf_op jit(solution)/shard_map/dot_general | solution.py:38
  (11 shorter events, 0.1 us)
Async XLA Ops:
  7.2 69.4 %all-gather.4.cloned.1.call-start = ((), (), s32[]{:S(2)}) async-start(), calls=%async_computation.2 | async-start | bytes 3932160 | tf_op jit(solution)/shard_map/all_gather | solution.py:29
  10.2 290.9 %all-gather.6.cloned.1.call-start = ((), (), s32[]{:S(2)}) async-start(), calls=%async_computation.3 | async-start | bytes 28311552 | tf_op jit(solution)/shard_map/all_gather | solution.py:32
  11.0 329.1 %reduce-scatter.2.cloned.1.call-start = ((), (), s32[]{:S(2)}) async-start(), calls=%async_computation.4 | async-start | bytes 1966080 | tf_op jit(solution)/shard_map/reduce_scatter | solution.py:35
  311.9 0.9 copy-start
  311.9 28.3 %copy-start.1 = (f32[1536]{0:T(1024)S(1)}, f32[1536]{0:T(1024)}, u32[]{:S(2)}) copy-start(f32[1536]{0:T(1024)} %param.7) | copy-start | bytes 18436
  311.9 28.3 %copy-start.2 = (f32[1536]{0:T(1024)S(1)}, f32[1536]{0:T(1024)}, u32[]{:S(2)}) copy-start(f32[1536]{0:T(1024)} %param.8) | copy-start | bytes 18436
  311.9 119.2 %all-gather.8.cloned.1.call-start = ((), (), s32[]{:S(2)}) async-start(), calls=%async_computation.5 | async-start | bytes 1769472 | tf_op jit(solution)/shard_map/all_gather | solution.py:36
Sparse Core Ops, SparseCore 0:
  10.3 66.1 all-gather.3
  78.1 222.9 all-gather.5
  312.0 28.0 reduce-scatter.1
  342.4 31.9 all-gather.7
where the time goes:
time: 449 us
  waiting for transfers between devices  298 us (66%)
  blocking collectives  101 us (22%)
  matrix products  21.6 us (5%)
  between operations  13.8 us (3%)
  other arithmetic  7.25 us (2%)
  local copies, waits for them, and re-layouts  7.21 us (2%)
    all_gather x1, waiting for transfers between devices, on_device(): lax.all_gather(up_weight, 'gx', axis=1, tiled=True)[0]  225 us
    all_gather x1, waiting for transfers between devices, on_device(): grad_rows = lax.all_gather(grad_local, 'gy', axis=0, tiled=True)  65.5 us
    all_to_all x1, blocking collectives, on_device(): lax.all_to_all(grad_rows, 'gx', split_axis=1, concat_axis=0, tiled=True)  46.1 us
    psum x1, blocking collectives, on_device(): lax.psum((jnp.sum(grad_normed * x_hat, axis=0), jnp.sum(grad_normed, axis...  22.9 us
    psum x1, blocking collectives, on_device(): lax.psum((jnp.sum(scaled, axis=1), jnp.sum(scaled * x_hat, axis=1)), 'gy')  11.7 us
    psum x1, blocking collectives, on_device(): totals = lax.psum(jnp.sum(widened, axis=1), 'gy')  11.7 us
    dot_general x1, matrix products, on_device(): lax.dot_general(grad_cols, normed_all, (((0,), (0,)), ((), ())), preferre...  10.9 us
    dot_general x1, matrix products, on_device(): jnp.dot(grad_rows, lax.all_gather(up_weight, 'gx', axis=1, tiled=True)[0]...  10.7 us
  transfers between devices with their start and end apart: 4, of which 3 were waited for; matrix products, arithmetic and copies ran while one was open for 2% of the time, Pallas kernels for 0%

commit v1 on v0

--- a/solution.py
+++ b/solution.py
@@ -27,14 +27,12 @@
     )
     grad_local = (grad_act.astype(jnp.float32) * slopes).astype(jnp.bfloat16)
     grad_rows = lax.all_gather(grad_local, "gy", axis=0, tiled=True)
-    partial_value = jnp.dot(
-        grad_rows,
-        lax.all_gather(up_weight, "gx", axis=1, tiled=True)[0],
-        preferred_element_type=jnp.float32,
+    grad_cols = lax.all_to_all(grad_rows, "gx", split_axis=1, concat_axis=0, tiled=True)
+    partial_value = jnp.dot(grad_cols, up_weight[0], preferred_element_type=jnp.float32)
+    grad_normed = lax.psum_scatter(
+        partial_value, ("gx", "gz"), scatter_dimension=0, tiled=True
     )
-    grad_normed = lax.psum_scatter(partial_value, "gz", scatter_dimension=0, tiled=True)
     normed_all = lax.all_gather(normed, ("gx", "gz"), axis=0, tiled=True)
-    grad_cols = lax.all_to_all(grad_rows, "gx", split_axis=1, concat_axis=0, tiled=True)
     weight_block = lax.dot_general(
         grad_cols, normed_all, (((0,), (0,)), ((), ())), preferred_element_type=jnp.float32
     )

time: 449 us -> 233 us (0.52)
  waiting for transfers between devices: 298 us -> 90.5 us
  blocking collectives: 101 us -> 93.5 us
    all_gather x1 -> x0, waiting for transfers between devices: 225 us -> none  [on_device(): lax.all_gather(up_weight, 'gx', axis=1, tiled=True)[0]]
    reduce_scatter x1, waiting for transfers between devices: 6.92 us -> 24.1 us  [on_device(): lax.psum_scatter(partial_value, ('gx', 'gz'), scatter_dimension=0, tiled=...]
    all_to_all x1, blocking collectives: 46.1 us -> 39.8 us  [on_device(): lax.all_to_all(grad_rows, 'gx', split_axis=1, concat_axis=0, tiled=True)]
  transfers between devices with their start and end apart: 4 -> 3, of which waited for: 3 -> 2; matrix products, arithmetic and copies ran while one was open for 2% -> 1% of each run, Pallas kernels for 0% -> 0%
where the time goes in v1:
time: 233 us; the launch traced here: 232 us
  blocking collectives  93.5 us (40%)
  waiting for transfers between devices  90.5 us (39%)
  matrix products  20.1 us (9%)
  between operations  13.8 us (6%)
  other arithmetic  7.25 us (3%)
  local copies, waits for them, and re-layouts  7.21 us (3%)
    all_gather x1, waiting for transfers between devices, on_device(): grad_rows = lax.all_gather(grad_local, 'gy', axis=0, tiled=True)  66.3 us
    all_to_all x1, blocking collectives, on_device(): lax.all_to_all(grad_rows, 'gx', split_axis=1, concat_axis=0, tiled=True)  39.8 us
    reduce_scatter x1, waiting for transfers between devices, on_device(): lax.psum_scatter(partial_value, ('gx', 'gz'), scatter_dimension=0, tiled=...  24.1 us
    psum x1, blocking collectives, on_device(): lax.psum((jnp.sum(grad_normed * x_hat, axis=0), jnp.sum(grad_normed, axis...  23.2 us
    psum x1, blocking collectives, on_device(): lax.psum((jnp.sum(scaled, axis=1), jnp.sum(scaled * x_hat, axis=1)), 'gy')  11.7 us
    dot_general x1, matrix products, on_device(): lax.dot_general(grad_cols, normed_all, (((0,), (0,)), ((), ())), preferre...  10.9 us
    psum x1, blocking collectives, on_device(): totals = lax.psum(jnp.sum(widened, axis=1), 'gy')  9.43 us
    psum x1, blocking collectives, on_device(): row_var = lax.psum(jnp.sum(centred * centred, axis=1), 'gy') / D  9.37 us
  transfers between devices with their start and end apart: 3, of which 2 were waited for; matrix products, arithmetic and copies ran while one was open for 1% of the time, Pallas kernels for 0%

profile of v1, /device:TPU:0, one launch (start us, length us, event | category | flops | bytes accessed | tf_op | source)
XLA Modules:
  0.0 232.5 jit_solution(9333573681793794145)
XLA Ops:
  7.2 0.0 all-gather.3.cloned.1.call-start
  7.2 3.0 %fusion.9 = bf16[64,6144]{1,0:T(8,128)(2,1)} fusion(bf16[64,6144]{1,0:T(8,128)(2,1)} %param.9, bf16[64,6144]{1,0:T(8,128)(2,1)} %param.10), kind=kLoop, calls=%fused_computation.14 | loop fusion | flops 4718592 | bytes 2359296 | tf_op jit(solution)/shard_map/convert_element_type | solution.py:28
  10.2 0.0 all-gather.3.cloned.1.call-update
  10.2 0.0 reduce-scatter.2.cloned.1.call-start
  10.3 66.3 %all-gather.3.cloned.1.call-done = bf16[256,6144]{1,0:T(8,128)(2,1)} async-done(((bf16[64,6144]{1,0:T(8,128)(2,1)}), bf16[256,6144]{1,0:T(8,128)(2,1)}) %all-gather.3.cloned.1.call-update) | async-done | bytes 3145744 | tf_op jit(solution)/shard_map/all_gather | solution.py:29
  76.5 3.2 %copy.13 = bf16[256,6144]{0,1:T(8,128)(2,1)S(1)} copy(bf16[256,6144]{1,0:T(8,128)(2,1)} %all-gather.3.cloned.1.call-done) | data formatting | bytes 6291456 | tf_op jit(solution)/shard_map/all_gather | solution.py:29
  79.7 39.8 %all_to_all.19 = bf16[256,2,3072]{0,2,1:T(8,128)(2,1)} all-to-all(bf16[256,2,3072]{0,2,1:T(8,128)(2,1)S(1)} %bitcast.11), channel_id=1, replica_groups=mesh['gx'=2,'gy'=4,'gz'=4] {'gx'}, dimensions={1} | all-to-all | bytes 6291456 | tf_op jit(solution)/shard_map/all_to_all | solution.py:30
  119.5 3.2 %copy.14 = bf16[2,256,3072]{2,1,0:T(8,128)(2,1)S(1)} copy(bf16[2,256,3072]{1,2,0:T(8,128)(2,1)} %bitcast.12) | data formatting | bytes 6291456 | tf_op jit(solution)/shard_map/all_to_all | solution.py:30
  122.7 9.2 %fusion = f32[512,1536]{1,0:T(8,128)} fusion(bf16[512,3072]{1,0:T(8,128)(2,1)S(1)} %bitcast.13, bf16[1,3072,1536]{2,1,0:T(8,128)(2,1)} %param.11), kind=kOutput, calls=%fused_computation.1 | convolution fusion | flops 4831838208 | bytes 15728640 | tf_op jit(solution)/shard_map/dot_general | solution.py:31
  131.9 0.0 reduce-scatter.2.cloned.1.call-update
  131.9 0.0 all-gather.5.cloned.1.call-start
  132.0 0.8 copy-done
  132.8 0.1 convert_reduce_fusion
  133.0 9.4 %psum.42 = f32[64]{0:T(128)S(1)} all-reduce(f32[64]{0:T(128)S(1)} %convert_reduce_fusion), channel_id=1, replica_groups=mesh['gx'=2,'gy'=4,'gz'=4] {'gy'}, use_global_device_ids=true, to_apply=%region_1.0 | all-reduce | flops 64 | bytes 512 | tf_op jit(solution)/shard_map/psum | solution.py:16
  142.4 0.2 fusion.23
  142.6 9.4 %psum.43 = f32[64]{0:T(128)S(1)} all-reduce(f32[64]{0:T(128)S(1)} %fusion.23), channel_id=1, replica_groups=mesh['gx'=2,'gy'=4,'gz'=4] {'gy'}, use_global_device_ids=true, to_apply=%region_3.0 | all-reduce | flops 64 | bytes 512 | tf_op jit(solution)/shard_map/psum | solution.py:19
  152.0 24.1 %reduce-scatter.2.cloned.1.call-done = f32[64,1536]{1,0:T(8,128)} async-done(((f32[512,1536]{1,0:T(8,128)}), f32[64,1536]{1,0:T(8,128)}) %reduce-scatter.2.cloned.1.call-update) | async-done | bytes 393232 | tf_op jit(solution)/shard_map/reduce_scatter | solution.py:32
  176.1 0.0 copy-done.2
  176.1 2.0 fusion.20
  178.2 0.0 all-gather.5.cloned.1.call-update
  178.2 11.7 %all-reduce.1 = (f32[64]{0:T(128)S(1)}, f32[64]{0:T(128)S(1)}) all-reduce(f32[64]{0:T(128)S(1)} %get-tuple-element.5, f32[64]{0:T(128)S(1)} %get-tuple-element.6), channel_id=1, replica_groups=mesh['gx'=2,'gy'=4,'gz'=4] {'gy'}, use_global_device_ids=true, to_apply=%region_8.0 | all-reduce | flops 128 | bytes 1024 | tf_op jit(solution)/shard_map/psum | solution.py:44
  189.9 23.2 %all-reduce = (f32[1536]{0:T(1024)}, f32[1536]{0:T(1024)}) all-reduce(f32[1536]{0:T(1024)S(1)} %get-tuple-element.4, f32[1536]{0:T(1024)S(1)} %get-tuple-element.7), channel_id=1, replica_groups=mesh['gx'=2,'gy'=4,'gz'=4] {'gx','gz'}, use_global_device_ids=true, to_apply=%region_10.0 | all-reduce | flops 3072 | bytes 24576 | tf_op jit(solution)/shard_map/psum | solution.py:40
  213.2 1.9 fusion.19
  215.0 10.9 %convolution_bitcast_fusion = f32[1,3072,1536]{2,1,0:T(8,128)} fusion(bf16[512,3072]{1,0:T(8,128)(2,1)S(1)} %bitcast.14, bf16[512,1536]{1,0:T(8,128)(2,1)} %all-gather.5.cloned.1.call-done), kind=kOutput, calls=%fused_computation | convolution fusion | flops 4831838208 | bytes 23592960 | tf_op jit(solution)/shard_map/dot_general | solution.py:36
  (8 shorter events, 0.0 us)
Async XLA Ops:
  7.2 69.4 %all-gather.3.cloned.1.call-start = ((), (), s32[]{:S(2)}) async-start(), calls=%async_computation.2 | async-start | bytes 3932160 | tf_op jit(solution)/shard_map/all_gather | solution.py:29
  10.2 165.9 %reduce-scatter.2.cloned.1.call-start = ((), (), s32[]{:S(2)}) async-start(), calls=%async_computation.3 | async-start | bytes 3538944 | tf_op jit(solution)/shard_map/reduce_scatter | solution.py:32
  131.9 0.9 copy-start
  131.9 44.2 %copy-start.1 = (f32[1536]{0:T(1024)S(1)}, f32[1536]{0:T(1024)}, u32[]{:S(2)}) copy-start(f32[1536]{0:T(1024)} %param.7) | copy-start | bytes 18436
  131.9 44.2 %copy-start.2 = (f32[1536]{0:T(1024)S(1)}, f32[1536]{0:T(1024)}, u32[]{:S(2)}) copy-start(f32[1536]{0:T(1024)} %param.8) | copy-start | bytes 18436
  131.9 83.1 %all-gather.5.cloned.1.call-start = ((), (), s32[]{:S(2)}) async-start(), calls=%async_computation.4 | async-start | bytes 1769472 | tf_op jit(solution)/shard_map/all_gather | solution.py:35
Sparse Core Ops, SparseCore 0:
  10.3 66.1 all-gather.2
  132.0 44.0 reduce-scatter.1
  178.6 25.7 all-gather.4

commit v2 on v1

v2 whole, which is shorter than its diff:
```python
import functools

import jax
import jax.numpy as jnp
from jax import lax
from jax.experimental import pallas as pl
from jax.experimental.pallas import tpu as pltpu
from jax.sharding import PartitionSpec as P

MESH = pl.DeviceIdType.MESH
LANES = 128
SUB = 8
CHUNK = 256

epsilon = 1e-05
root_half = 0.7071067811865476
gauss_norm = 0.3989422804014327


def to_tile(pad, first, second, rows):
    lane = lax.broadcasted_iota(jnp.int32, (rows, LANES), 1)
    pad[...] = jnp.zeros_like(pad)
    pad[:rows, :] = jnp.where(lane == 0, first, jnp.where(lane == 1, second, 0.0))
    return pad[...].T[:SUB, :]


def to_columns(pad, tile, rows):
    pad[...] = jnp.zeros_like(pad)
    pad[:SUB, :] = tile
    flipped = pad[...].T
    return flipped[:rows, 0:1], flipped[:rows, 1:2]


def kernel(
    sizes,
    inputs, gain, bias, grad_local, weight,
    cols_out, normed_out, grad_inputs, grad_sums,
    w_buf, cols, part_send, part_recv, x_hat, grad_normed, normed_own, sums, pad, stat_a, stat_b,
    w_sem, own_sem, out_sem, z_recv, right_send, left_send, x_send,
    stat_send, stat_recv, norm_send, norm_recv, norm_own_sem, part_ssem, part_rsem, part_own_sem,
    sums_send, sums_recv, last_send, last_recv,
):
    n_gx, n_gy, n_gz, rows, rows_in, width, depth = sizes
    ratio = rows // rows_in
    plane = n_gx * n_gz
    g, p, t = lax.axis_index("gx"), lax.axis_index("gy"), lax.axis_index("gz")
    me = g * n_gz + t
    model = width * n_gy

    def line_peer(i):
        return lax.rem(p + i, n_gy)

    def plane_peer(i):
        other = lax.rem(me + i, plane)
        return other, {"gx": other // n_gz, "gz": lax.rem(other, n_gz)}

    def slot(q, u):
        return q * n_gx + u

    barrier = pltpu.get_barrier_semaphore()
    for i in range(1, n_gy):
        pl.semaphore_signal(barrier, inc=1, device_id={"gy": line_peer(i)}, device_id_type=MESH)

    @pl.loop(1, plane)
    def _(i):
        pl.semaphore_signal(barrier, inc=1, device_id=plane_peer(i)[1], device_id_type=MESH)

    own = pltpu.make_async_copy(
        grad_local.at[:, pl.ds(pl.multiple_of(g * depth, LANES), depth)], cols.at[p, g], own_sem
    )
    own.start()
    w_copy = pltpu.make_async_copy(weight, w_buf, w_sem)
    w_copy.start()

    widened = inputs[...].astype(jnp.float32)
    mean_here = jnp.sum(widened, axis=1, keepdims=True) / width
    centred = widened - mean_here
    square_here = jnp.sum(centred * centred, axis=1, keepdims=True)
    stat_a[p] = to_tile(pad, mean_here, square_here, rows_in)

    pl.semaphore_wait(barrier, n_gy - 1 + plane - 1)

    def tile_copy(buf, i, ssem, rsem, source):
        return pltpu.make_async_remote_copy(
            src_ref=buf.at[source], dst_ref=buf.at[source],
            send_sem=ssem.at[line_peer(i)], recv_sem=rsem.at[source],
            device_id={"gy": line_peer(i)}, device_id_type=MESH,
        )

    for i in range(1, n_gy):
        tile_copy(stat_a, i, stat_send, stat_recv, p).start()

    def x_copy(i, source):
        u = lax.rem(g + i, n_gx)
        return pltpu.make_async_remote_copy(
            src_ref=grad_local.at[:, pl.ds(pl.multiple_of(u * depth, LANES), depth)],
            dst_ref=cols.at[p, source],
            send_sem=x_send.at[u], recv_sem=z_recv.at[slot(p, source)],
            device_id={"gx": u}, device_id_type=MESH,
        )

    def z_copy(q, u, step, sems):
        return pltpu.make_async_remote_copy(
            src_ref=cols.at[q, u], dst_ref=cols.at[q, u],
            send_sem=sems.at[slot(q, u)], recv_sem=z_recv.at[slot(q, u)],
            device_id={"gy": lax.rem(p + step + n_gy, n_gy)}, device_id_type=MESH,
        )

    def out_copy(q, u):
        return pltpu.make_async_copy(cols.at[q, u], cols_out.at[u, q], out_sem.at[slot(q, u)])

    def pass_right(q, u):
        @pl.when(p + 1 < n_gy)
        def _():
            z_copy(q, u, 1, right_send).start()

    def pass_left(q, u):
        @pl.when(p >= 1)
        def _():
            z_copy(q, u, -1, left_send).start()

    for i in range(1, n_gx):
        x_copy(i, g).start()
    own.wait()
    pass_right(p, g)
    pass_left(p, g)
    out_copy(p, g).start()

    for i in range(1, n_gy):
        tile_copy(stat_a, i, stat_send, stat_recv, line_peer(i)).wait_recv()
    columns = [to_columns(pad, stat_a[q], rows_in) for q in range(n_gy)]
    mean = sum(c[0] for c in columns) / n_gy
    total = sum(c[1] + width * (c[0] - mean) * (c[0] - mean) for c in columns)
    inv_std = lax.rsqrt(total / model + epsilon)
    x_hat[...] = (inputs[...].astype(jnp.float32) - mean) * inv_std
    normed_own[...] = (x_hat[...] * gain[...] + bias[...]).astype(jnp.bfloat16)

    def norm_copy(i, source):
        other, where = plane_peer(i)
        return pltpu.make_async_remote_copy(
            src_ref=normed_own, dst_ref=normed_out.at[source],
            send_sem=norm_send.at[other], recv_sem=norm_recv.at[source],
            device_id=where, device_id_type=MESH,
        )

    @pl.loop(1, plane)
    def _(i):
        norm_copy(i, me).start()

    norm_own = pltpu.make_async_copy(normed_own, normed_out.at[me], norm_own_sem)
    norm_own.start()

    for i in range(1, n_gx):
        u = lax.rem(g + i, n_gx)
        x_copy(i, u).wait_recv()
        pass_right(p, u)
        pass_left(p, u)
        out_copy(p, u).start()
    w_copy.wait()

    def part_copy(q, u, j, source):
        owner = q * ratio + j
        return pltpu.make_async_remote_copy(
            src_ref=part_send.at[q, u, j], dst_ref=part_recv.at[source],
            send_sem=part_ssem.at[u * n_gz + owner], recv_sem=part_rsem.at[source],
            device_id={"gx": u, "gz": owner}, device_id_type=MESH,
        )

    def part_keep(q, u, j):
        return pltpu.make_async_copy(part_send.at[q, u, j], part_recv.at[me], part_own_sem)

    def multiply(q):
        @pl.loop(0, width // CHUNK)
        def _(c):
            span = pl.ds(pl.multiple_of(c * CHUNK, CHUNK), CHUNK)
            block = cols[q].reshape(n_gx * rows, depth)
            value = jnp.dot(block, w_buf[:, span], preferred_element_type=jnp.float32)
            part_send[q, :, :, :, span] = value.astype(jnp.bfloat16).reshape(
                n_gx, ratio, rows_in, CHUNK
            )

        for u in range(n_gx):
            for j in range(ratio):
                mine = jnp.logical_and(u == g, q * ratio + j == t)

                @pl.when(mine)
                def _():
                    part_keep(q, u, j).start()

                @pl.when(jnp.logical_not(mine))
                def _():
                    part_copy(q, u, j, me).start()

    multiply(p)

    @pl.loop(1, n_gy)
    def _(s):
        for k in range(n_gx):
            u = lax.rem(g + k, n_gx)

            @pl.when(p - s >= 0)
            def _():
                z_copy(p - s, u, 1, right_send).wait_recv()
                pass_right(p - s, u)
                out_copy(p - s, u).start()

            @pl.when(p + s < n_gy)
            def _():
                z_copy(p + s, u, -1, left_send).wait_recv()
                pass_left(p + s, u)
                out_copy(p + s, u).start()

        @pl.loop(0, 2)
        def _(side):
            q = p + (2 * side - 1) * s

            @pl.when(jnp.logical_and(q >= 0, q < n_gy))
            def _():
                multiply(q)

    part_keep(0, 0, 0).wait()

    @pl.loop(1, plane)
    def _(i):
        other, where = plane_peer(i)
        pltpu.make_async_remote_copy(
            src_ref=part_send.at[0, 0, 0], dst_ref=part_recv.at[other],
            send_sem=part_ssem.at[other], recv_sem=part_rsem.at[other],
            device_id=where, device_id_type=MESH,
        ).wait_recv()

    row_sum = jnp.zeros((rows_in, 1), jnp.float32)
    row_dot = jnp.zeros((rows_in, 1), jnp.float32)
    for start in range(0, width, CHUNK):
        span = slice(start, start + CHUNK)
        block = lax.fori_loop(
            0, plane,
            lambda i, acc: acc + part_recv[i, :, span].astype(jnp.float32),
            jnp.zeros((rows_in, CHUNK), jnp.float32),
        )
        grad_normed[:, span] = block
        hat = x_hat[:, span]
        sums[me, 0:1, span] = jnp.sum(block * hat, axis=0, keepdims=True)
        sums[me, 1:2, span] = jnp.sum(block, axis=0, keepdims=True)
        scaled = block * gain[:, span]
        row_sum = row_sum + jnp.sum(scaled, axis=1, keepdims=True)
        row_dot = row_dot + jnp.sum(scaled * hat, axis=1, keepdims=True)
    stat_b[p] = to_tile(pad, row_sum, row_dot, rows_in)
    for i in range(1, n_gy):
        tile_copy(stat_b, i, last_send, last_recv, p).start()

    def sums_copy(i, source):
        other, where = plane_peer(i)
        return pltpu.make_async_remote_copy(
            src_ref=sums.at[source], dst_ref=sums.at[source],
            send_sem=sums_send.at[other], recv_sem=sums_recv.at[source],
            device_id=where, device_id_type=MESH,
        )

    @pl.loop(1, plane)
    def _(i):
        sums_copy(i, me).start()

    for i in range(1, n_gy):
        tile_copy(stat_b, i, last_send, last_recv, line_peer(i)).wait_recv()
    both = stat_b[0]
    for q in range(1, n_gy):
        both = both + stat_b[q]
    grad_sum, grad_dot = to_columns(pad, both, rows_in)
    for start in range(0, width, CHUNK):
        span = slice(start, start + CHUNK)
        scaled = grad_normed[:, span] * gain[:, span]
        grad_inputs[:, span] = (
            inv_std * (scaled - grad_sum / model - x_hat[:, span] * (grad_dot / model))
        ).astype(jnp.bfloat16)

    @pl.loop(1, plane)
    def _(i):
        sums_copy(i, plane_peer(i)[0]).wait_recv()

    grad_sums[...] = lax.fori_loop(
        0, plane, lambda i, acc: acc + sums[i], jnp.zeros((2, width), jnp.float32)
    )

    norm_own.wait()

    @pl.loop(1, plane)
    def _(i):
        other, where = plane_peer(i)
        norm_copy(i, me).wait_send()
        norm_copy(i, other).wait_recv()
        sums_copy(i, me).wait_send()
        pltpu.make_async_remote_copy(
            src_ref=part_send.at[0, 0, 0], dst_ref=part_recv.at[me],
            send_sem=part_ssem.at[other], recv_sem=part_rsem.at[me],
            device_id=where, device_id_type=MESH,
        ).wait_send()

    for i in range(1, n_gy):
        tile_copy(stat_a, i, stat_send, stat_recv, p).wait_send()
        tile_copy(stat_b, i, last_send, last_recv, p).wait_send()
    for i in range(1, n_gx):
        x_copy(i, g).wait_send()

    @pl.loop(0, n_gy)
    def _(q):
        for u in range(n_gx):
            out_copy(q, u).wait()

            @pl.when(jnp.logical_and(q <= p, p + 1 < n_gy))
            def _():
                z_copy(q, u, 1, right_send).wait_send()

            @pl.when(jnp.logical_and(q >= p, p >= 1))
            def _():
                z_copy(q, u, -1, left_send).wait_send()


def on_device(shape, inputs, norm_gain, norm_bias, pre_act, grad_act, up_weight):
    n_gx, n_gy, n_gz = shape["gx"], shape["gy"], shape["gz"]
    plane = n_gx * n_gz
    rows_in, width = inputs.shape
    rows = pre_act.shape[0]
    depth = up_weight.shape[1]
    ratio = rows // rows_in
    pre_float = pre_act.astype(jnp.float32)
    slopes = (
        0.5 * (1.0 + jax.scipy.special.erf(pre_float * root_half))
        + pre_float * jnp.exp(-0.5 * pre_float * pre_float) * gauss_norm
    )
    grad_local = (grad_act.astype(jnp.float32) * slopes).astype(jnp.bfloat16)
    whole, vmem = pl.BlockSpec(memory_space=pl.ANY), pl.BlockSpec(memory_space=pltpu.VMEM)
    dma = pltpu.SemaphoreType.DMA
    bf16, f32 = jnp.bfloat16, jnp.float32
    slots = n_gx * n_gy
    grad_cols, normed_all, grad_inputs, grad_sums = pl.pallas_call(
        functools.partial(kernel, (n_gx, n_gy, n_gz, rows, rows_in, width, depth)),
        out_shape=(
            jax.ShapeDtypeStruct((n_gx, n_gy, rows, depth), bf16),
            jax.ShapeDtypeStruct((plane, rows_in, width), bf16),
            jax.ShapeDtypeStruct((rows_in, width), bf16),
            jax.ShapeDtypeStruct((2, width), f32),
        ),
        in_specs=[vmem, vmem, vmem, whole, whole],
        out_specs=(whole, whole, vmem, vmem),
        scratch_shapes=[
            pltpu.VMEM((depth, width), bf16),
            pltpu.VMEM((n_gy, n_gx, rows, depth), bf16),
            pltpu.VMEM((n_gy, n_gx, ratio, rows_in, width), bf16),
            pltpu.VMEM((plane, rows_in, width), bf16),
            pltpu.VMEM((rows_in, width), f32),
            pltpu.VMEM((rows_in, width), f32),
            pltpu.VMEM((rows_in, width), bf16),
            pltpu.VMEM((plane, 2, width), f32),
            pltpu.VMEM((LANES, LANES), f32),
            pltpu.VMEM((n_gy, SUB, LANES), f32),
            pltpu.VMEM((n_gy, SUB, LANES), f32),
            dma, dma, dma((slots,)), dma((slots,)), dma((slots,)), dma((slots,)), dma((n_gx,)),
            dma((n_gy,)), dma((n_gy,)), dma((plane,)), dma((plane,)), dma,
            dma((plane,)), dma((plane,)), dma,
            dma((plane,)), dma((plane,)), dma((n_gy,)), dma((n_gy,)),
        ],
        compiler_params=pltpu.CompilerParams(
            collective_id=0, has_side_effects=True, vmem_limit_bytes=60 * 1024 * 1024
        ),
    )(inputs, norm_gain[None], norm_bias[None], grad_local, up_weight[0])
    tokens = slots * rows
    weight_block = lax.dot_general(
        grad_cols.reshape(tokens, depth),
        normed_all.reshape(tokens, width),
        (((0,), (0,)), ((), ())),
        preferred_element_type=jnp.float32,
    )
    return grad_inputs, grad_sums[0], grad_sums[1], weight_block.reshape(up_weight.shape)


def solution(mesh):
    in_specs = (
        P(("gx", "gz"), "gy"),
        P("gy"),
        P("gy"),
        P(("gx", "gy"), "gz"),
        P(("gx", "gy"), "gz"),
        P("gz", "gx", "gy"),
    )
    out_specs = (P(("gx", "gz"), "gy"), P("gy"), P("gy"), P("gz", "gx", "gy"))
    return jax.shard_map(
        functools.partial(on_device, dict(mesh.shape)),
        mesh=mesh, in_specs=in_specs, out_specs=out_specs, check_vma=False,
    )
```

time: 233 us -> 94.6 us (0.41)
  blocking collectives: 93.5 us -> 0 us
  waiting for transfers between devices: 90.5 us -> 0 us
  Pallas kernels: 0 us -> 76.8 us
  between operations: 13.8 us -> 0.68 us
  matrix products: 20.1 us -> 11.4 us
  local copies, waits for them, and re-layouts: 7.21 us -> 2.52 us
  other arithmetic: 7.25 us -> 3 us
    pallas_call x0 -> x1, Pallas kernels: none -> 76.8 us  [on_device(): pl.pallas_call(functools.partial(kernel, (n_gx, n_gy, n_gz, rows, rows_in...]
    all_gather x2 -> x0, waiting for transfers between devices: 66.3 us -> none  [the longest x1 66.3 us: on_device(): grad_rows = lax.all_gather(grad_local, 'gy', axis=0, tiled=True)]
    psum x4 -> x0, blocking collectives: 53.7 us -> none  [the longest x1 23.2 us: on_device(): lax.psum((jnp.sum(grad_normed * x_hat, axis=0), jnp.sum(grad_normed, axis...]
    all_to_all x1 -> x0, blocking collectives: 39.8 us -> none  [on_device(): lax.all_to_all(grad_rows, 'gx', split_axis=1, concat_axis=0, tiled=True)]
    reduce_scatter x1 -> x0, waiting for transfers between devices: 24.1 us -> none  [on_device(): lax.psum_scatter(partial_value, ('gx', 'gz'), scatter_dimension=0, tiled=...]
    dot_general x2 -> x1, matrix products: 20.1 us -> 11.4 us  [on_device(): lax.dot_general(grad_cols.reshape(tokens, depth), normed_all.reshape(toke...]
    all_to_all x1 -> x0, local copies, waits for them, and re-layouts: 3.18 us -> none  [on_device(): lax.all_to_all(grad_rows, 'gx', split_axis=1, concat_axis=0, tiled=True)]
    all_gather x1 -> x0, local copies, waits for them, and re-layouts: 3.17 us -> none  [on_device(): grad_rows = lax.all_gather(grad_local, 'gy', axis=0, tiled=True)]
  transfers between devices with their start and end apart: 3 -> 0, of which waited for: 2 -> 0; matrix products, arithmetic and copies ran while one was open for 1% -> 0% of each run, Pallas kernels for 0% -> 0%
where the time goes in v2:
time: 94.6 us; the launch traced here: 94.4 us
  Pallas kernels  76.8 us (81%)
  matrix products  11.4 us (12%)
  other arithmetic  3 us (3%)
  local copies, waits for them, and re-layouts  2.52 us (3%)
    pallas_call x1, Pallas kernels, on_device(): pl.pallas_call(functools.partial(kernel, (n_gx, n_gy, n_gz, rows, rows_in...  76.8 us
    dot_general x1, matrix products, on_device(): lax.dot_general(grad_cols.reshape(tokens, depth), normed_all.reshape(toke...  11.4 us
    convert_element_type x1, other arithmetic, on_device(): grad_local = (grad_act.astype(jnp.float32) * slopes).astype(jnp.bfloat16)  3 us

profile of v2, /device:TPU:0, one launch (start us, length us, event | category | flops | bytes accessed | tf_op | source)
XLA Modules:
  0.0 94.4 jit_solution(15310430616839873949)
XLA Ops:
  0.6 0.0 copy-start.2
  0.6 0.0 copy-start.3
  0.7 3.0 %fusion.7.grad_local = bf16[64,6144]{1,0:T(8,128)(2,1)} fusion(bf16[64,6144]{1,0:T(8,128)(2,1)} %param.9, bf16[64,6144]{1,0:T(8,128)(2,1)} %param.10), kind=kLoop, calls=%fused_computation.12 | loop fusion | flops 4718592 | bytes 2359296 | tf_op jit(solution)/shard_map/convert_element_type | solution.py:331
  3.7 0.0 copy-done.2
  3.7 0.6 broadcast_in_dim.6.gain
  4.3 0.0 copy-done.3
  4.3 0.6 broadcast_in_dim.7.bias
  4.9 76.8 %shard_map.93 = (bf16[2,4,64,3072]{3,2,1,0:T(8,128)(2,1)}, bf16[8,64,1536]{2,1,0:T(8,128)(2,1)}, bf16[64,1536]{1,0:T(8,128)(2,1)}, f32[2,1536]{1,0:T(2,128)}) custom-call(bf16[64,1536]{1,0:T(8,128)(2,1)} %inputs.1, f32[1,1536]{1,0:T(1,128)} %broadcast_in_dim.6.gain, f32[1,1536]{1,0:T(1,128)} %broadcast_in_dim.7.bias, bf16[64,6144]{1,0:T(8,128)(2,1)} %fusion.7.grad_local, ...), custom_call_target="tpu_custom_call" | custom-call | tf_op jit(solution)/shard_map/pallas_call | solution.py:336
  81.7 0.0 copy-start.1
  81.7 0.0 copy-start
  81.7 11.4 %convolution_bitcast_fusion = f32[1,3072,1536]{2,1,0:T(8,128)} fusion(bf16[512,3072]{1,0:T(8,128)(2,1)} %bitcast.8, bf16[512,1536]{1,0:T(8,128)(2,1)} %bitcast.9), kind=kOutput, calls=%fused_computation | convolution fusion | flops 4831838208 | bytes 23592960 | tf_op jit(solution)/shard_map/dot_general | solution.py:368
  93.1 0.0 copy-done.1
  93.1 0.6 slice_reduce_fusion
  93.7 0.0 copy-done
  93.7 0.7 copy.11
Async XLA Ops:
  0.6 3.0 %copy-start.2 = (f32[1536]{0:T(1024)S(1)}, f32[1536]{0:T(1024)}, u32[]{:S(2)}) copy-start(f32[1536]{0:T(1024)} %param.7) | copy-start | bytes 18436
  0.6 3.6 %copy-start.3 = (f32[1536]{0:T(1024)S(1)}, f32[1536]{0:T(1024)}, u32[]{:S(2)}) copy-start(f32[1536]{0:T(1024)} %param.8) | copy-start | bytes 18436
  81.7 11.4 %copy-start.1 = (f32[2,1536]{1,0:T(2,128)S(1)}, f32[2,1536]{1,0:T(2,128)}, u32[]{:S(2)}) copy-start(f32[2,1536]{1,0:T(2,128)} %get-tuple-element.9) | copy-start | bytes 36868
  81.7 12.1 %copy-start = (bf16[64,1536]{1,0:T(8,128)(2,1)S(1)}, bf16[64,1536]{1,0:T(8,128)(2,1)}, u32[]{:S(2)}) copy-start(bf16[64,1536]{1,0:T(8,128)(2,1)} %get-tuple-element.18) | copy-start | bytes 589828

commit v3 on v2

v3 whole, which is shorter than its diff:
```python
import functools

import jax
import jax.numpy as jnp
from jax import lax
from jax.experimental import pallas as pl
from jax.experimental.pallas import tpu as pltpu
from jax.sharding import PartitionSpec as P

MESH = pl.DeviceIdType.MESH
LANES = 128
SUB = 8
CHUNK = 256
SEND = 512

epsilon = 1e-05
root_half = 0.7071067811865476
gauss_norm = 0.3989422804014327


def to_tile(pad, first, second, rows):
    lane = lax.broadcasted_iota(jnp.int32, (rows, LANES), 1)
    pad[...] = jnp.zeros_like(pad)
    pad[:rows, :] = jnp.where(lane == 0, first, jnp.where(lane == 1, second, 0.0))
    return pad[...].T[:SUB, :]


def to_columns(pad, tile, rows):
    pad[...] = jnp.zeros_like(pad)
    pad[:SUB, :] = tile
    flipped = pad[...].T
    return flipped[:rows, 0:1], flipped[:rows, 1:2]


def kernel(
    sizes,
    inputs, gain, bias, pre_act, grad_act, weight,
    cols_out, normed_out, grad_inputs, grad_gain, grad_bias,
    pre_buf, act_buf, stage, w_buf, cols, part_send, part_recv, x_hat, grad_normed, normed_own, sums, pad, stat_a, stat_b,
    pre_sem, act_sem, w_sem, out_sem, z_recv, right_send, left_send, x_send,
    stat_send, stat_recv, norm_send, norm_recv, norm_own_sem, part_ssem, part_rsem, part_own_sem,
    sums_send, sums_recv, last_send, last_recv,
):
    n_gx, n_gy, n_gz, rows, rows_in, width, depth = sizes
    ratio = rows // rows_in
    plane = n_gx * n_gz
    g, p, t = lax.axis_index("gx"), lax.axis_index("gy"), lax.axis_index("gz")
    me = g * n_gz + t
    model = width * n_gy

    def line_peer(i):
        return lax.rem(p + i, n_gy)

    def plane_peer(i):
        other = lax.rem(me + i, plane)
        return other, {"gx": other // n_gz, "gz": lax.rem(other, n_gz)}

    def slot(q, u):
        return q * n_gx + u

    def row(ref, span):
        return ref[span].reshape(1, -1)

    barrier = pltpu.get_barrier_semaphore()
    for i in range(1, n_gy):
        pl.semaphore_signal(barrier, inc=1, device_id={"gy": line_peer(i)}, device_id_type=MESH)

    @pl.loop(1, plane)
    def _(i):
        pl.semaphore_signal(barrier, inc=1, device_id=plane_peer(i)[1], device_id_type=MESH)

    def half(ref, u):
        return ref.at[:, pl.ds(pl.multiple_of(u * depth, LANES), depth)]

    loads = []
    for i in list(range(1, n_gx)) + [0]:
        u = lax.rem(g + i, n_gx)
        pair = (
            pltpu.make_async_copy(half(pre_act, u), pre_buf.at[u], pre_sem.at[u]),
            pltpu.make_async_copy(half(grad_act, u), act_buf.at[u], act_sem.at[u]),
        )
        for copy in pair:
            copy.start()
        loads.append((u, pair))
    w_copy = pltpu.make_async_copy(weight, w_buf, w_sem)
    w_copy.start()

    step = next(n for n in (384, 256, LANES) if depth % n == 0)

    def gelu_grad(u, pair, out):
        for copy in pair:
            copy.wait()

        @pl.loop(0, depth // step)
        def _(c):
            span = pl.ds(pl.multiple_of(c * step, step), step)
            pre = pre_buf[u, :, span].astype(jnp.float32)
            slopes = (
                0.5 * (1.0 + lax.erf(pre * root_half))
                + pre * jnp.exp(-0.5 * pre * pre) * gauss_norm
            )
            out[:, span] = (act_buf[u, :, span].astype(jnp.float32) * slopes).astype(jnp.bfloat16)

    for u, pair in loads[:-1]:
        gelu_grad(u, pair, stage.at[u])

    pl.semaphore_wait(barrier, n_gy - 1 + plane - 1)

    def tile_copy(buf, i, ssem, rsem, source):
        return pltpu.make_async_remote_copy(
            src_ref=buf.at[source], dst_ref=buf.at[source],
            send_sem=ssem.at[line_peer(i)], recv_sem=rsem.at[source],
            device_id={"gy": line_peer(i)}, device_id_type=MESH,
        )

    def x_copy(i, source):
        u = lax.rem(g + i, n_gx)
        return pltpu.make_async_remote_copy(
            src_ref=stage.at[u],
            dst_ref=cols.at[p, source],
            send_sem=x_send.at[u], recv_sem=z_recv.at[slot(p, source)],
            device_id={"gx": u}, device_id_type=MESH,
        )

    def z_copy(q, u, step, sems):
        return pltpu.make_async_remote_copy(
            src_ref=cols.at[q, u], dst_ref=cols.at[q, u],
            send_sem=sems.at[slot(q, u)], recv_sem=z_recv.at[slot(q, u)],
            device_id={"gy": lax.rem(p + step + n_gy, n_gy)}, device_id_type=MESH,
        )

    def out_copy(q, u):
        return pltpu.make_async_copy(cols.at[q, u], cols_out.at[u, q], out_sem.at[slot(q, u)])

    def pass_right(q, u):
        @pl.when(p + 1 < n_gy)
        def _():
            z_copy(q, u, 1, right_send).start()

    def pass_left(q, u):
        @pl.when(p >= 1)
        def _():
            z_copy(q, u, -1, left_send).start()

    for i in range(1, n_gx):
        x_copy(i, g).start()
    gelu_grad(loads[-1][0], loads[-1][1], cols.at[p, g])
    pass_right(p, g)
    pass_left(p, g)
    out_copy(p, g).start()

    widened = inputs[...].astype(jnp.float32)
    mean_here = jnp.sum(widened, axis=1, keepdims=True) / width
    centred = widened - mean_here
    square_here = jnp.sum(centred * centred, axis=1, keepdims=True)
    stat_a[p] = to_tile(pad, mean_here, square_here, rows_in)
    for i in range(1, n_gy):
        tile_copy(stat_a, i, stat_send, stat_recv, p).start()

    for i in range(1, n_gx):
        u = lax.rem(g + i, n_gx)
        x_copy(i, u).wait_recv()
        pass_right(p, u)
        pass_left(p, u)
        out_copy(p, u).start()
    for i in range(1, n_gy):
        tile_copy(stat_a, i, stat_send, stat_recv, line_peer(i)).wait_recv()
    columns = [to_columns(pad, stat_a[q], rows_in) for q in range(n_gy)]
    mean = sum(c[0] for c in columns) / n_gy
    total = sum(c[1] + width * (c[0] - mean) * (c[0] - mean) for c in columns)
    inv_std = lax.rsqrt(total / model + epsilon)
    x_hat[...] = (inputs[...].astype(jnp.float32) - mean) * inv_std
    normed_own[...] = (x_hat[...] * row(gain, slice(None)) + row(bias, slice(None))).astype(jnp.bfloat16)

    def norm_copy(i, source):
        other, where = plane_peer(i)
        return pltpu.make_async_remote_copy(
            src_ref=normed_own, dst_ref=normed_out.at[source],
            send_sem=norm_send.at[other], recv_sem=norm_recv.at[source],
            device_id=where, device_id_type=MESH,
        )

    @pl.loop(1, plane)
    def _(i):
        norm_copy(i, me).start()

    norm_own = pltpu.make_async_copy(normed_own, normed_out.at[me], norm_own_sem)
    norm_own.start()

    w_copy.wait()

    def part_copy(q, u, j, source, span):
        owner = q * ratio + j
        return pltpu.make_async_remote_copy(
            src_ref=part_send.at[q, u, j, :, span], dst_ref=part_recv.at[source, :, span],
            send_sem=part_ssem.at[u * n_gz + owner], recv_sem=part_rsem.at[source],
            device_id={"gx": u, "gz": owner}, device_id_type=MESH,
        )

    def multiply(q, units):
        count = n_gx if units is None else 1

        @pl.loop(0, width // SEND)
        def _(c):
            span = pl.ds(pl.multiple_of(c * SEND, SEND), SEND)
            block = cols[q].reshape(n_gx * rows, depth) if units is None else cols[q, units]
            for part in range(0, SEND, CHUNK):
                piece = pl.ds(pl.multiple_of(c * SEND + part, CHUNK), CHUNK)
                value = jnp.dot(block, w_buf[:, piece], preferred_element_type=jnp.float32)
                value = value.astype(jnp.bfloat16).reshape(count, ratio, rows_in, CHUNK)
                if units is None:
                    part_send[q, :, :, :, piece] = value
                else:
                    part_send[q, units, :, :, piece] = value[0]
            for u in range(n_gx) if units is None else [units]:
                for j in range(ratio):
                    mine = jnp.logical_and(u == g, q * ratio + j == t)

                    @pl.when(mine)
                    def _():
                        pltpu.make_async_copy(
                            part_send.at[q, u, j, :, span], part_recv.at[me, :, span], part_own_sem
                        ).start()

                    @pl.when(jnp.logical_not(mine))
                    def _():
                        part_copy(q, u, j, me, span).start()

    multiply(p, None)

    def take(s, k):
        u = lax.rem(g + k, n_gx)

        @pl.when(p - s >= 0)
        def _():
            z_copy(p - s, u, 1, right_send).wait_recv()
            pass_right(p - s, u)
            out_copy(p - s, u).start()

        @pl.when(p + s < n_gy)
        def _():
            z_copy(p + s, u, -1, left_send).wait_recv()
            pass_left(p + s, u)
            out_copy(p + s, u).start()

    @pl.loop(1, n_gy - 1)
    def _(s):
        for k in range(n_gx):
            take(s, k)

        @pl.loop(0, 2)
        def _(side):
            q = p + (2 * side - 1) * s

            @pl.when(jnp.logical_and(q >= 0, q < n_gy))
            def _():
                multiply(q, None)

    @pl.when(jnp.logical_or(p == 0, p == n_gy - 1))
    def _():
        @pl.loop(0, n_gx)
        def _(k):
            take(n_gy - 1, k)
            multiply(n_gy - 1 - p, lax.rem(g + k, n_gx))

    pltpu.make_async_copy(part_send.at[0, 0, 0], part_recv.at[me], part_own_sem).wait()

    @pl.loop(1, plane)
    def _(i):
        other, where = plane_peer(i)
        pltpu.make_async_remote_copy(
            src_ref=part_send.at[0, 0, 0], dst_ref=part_recv.at[other],
            send_sem=part_ssem.at[other], recv_sem=part_rsem.at[other],
            device_id=where, device_id_type=MESH,
        ).wait_recv()

    row_sum = jnp.zeros((rows_in, 1), jnp.float32)
    row_dot = jnp.zeros((rows_in, 1), jnp.float32)
    for start in range(0, width, CHUNK):
        span = slice(start, start + CHUNK)
        block = lax.fori_loop(
            0, plane,
            lambda i, acc: acc + part_recv[i, :, span].astype(jnp.float32),
            jnp.zeros((rows_in, CHUNK), jnp.float32),
            unroll=8,
        )
        grad_normed[:, span] = block
        hat = x_hat[:, span]
        sums[me, 0:1, span] = jnp.sum(block * hat, axis=0, keepdims=True)
        sums[me, 1:2, span] = jnp.sum(block, axis=0, keepdims=True)
        scaled = block * row(gain, span)
        row_sum = row_sum + jnp.sum(scaled, axis=1, keepdims=True)
        row_dot = row_dot + jnp.sum(scaled * hat, axis=1, keepdims=True)
    stat_b[p] = to_tile(pad, row_sum, row_dot, rows_in)
    for i in range(1, n_gy):
        tile_copy(stat_b, i, last_send, last_recv, p).start()

    def sums_copy(i, source):
        other, where = plane_peer(i)
        return pltpu.make_async_remote_copy(
            src_ref=sums.at[source], dst_ref=sums.at[source],
            send_sem=sums_send.at[other], recv_sem=sums_recv.at[source],
            device_id=where, device_id_type=MESH,
        )

    @pl.loop(1, plane)
    def _(i):
        sums_copy(i, me).start()

    for i in range(1, n_gy):
        tile_copy(stat_b, i, last_send, last_recv, line_peer(i)).wait_recv()
    both = stat_b[0]
    for q in range(1, n_gy):
        both = both + stat_b[q]
    grad_sum, grad_dot = to_columns(pad, both, rows_in)
    for start in range(0, width, CHUNK):
        span = slice(start, start + CHUNK)
        scaled = grad_normed[:, span] * row(gain, span)
        grad_inputs[:, span] = (
            inv_std * (scaled - grad_sum / model - x_hat[:, span] * (grad_dot / model))
        ).astype(jnp.bfloat16)

    @pl.loop(1, plane)
    def _(i):
        sums_copy(i, plane_peer(i)[0]).wait_recv()

    both = lax.fori_loop(
        0, plane, lambda i, acc: acc + sums[i], jnp.zeros((2, width), jnp.float32), unroll=8
    )
    grad_gain[...] = both[0]
    grad_bias[...] = both[1]

    norm_own.wait()

    @pl.loop(1, plane)
    def _(i):
        other, where = plane_peer(i)
        norm_copy(i, me).wait_send()
        norm_copy(i, other).wait_recv()
        sums_copy(i, me).wait_send()
        pltpu.make_async_remote_copy(
            src_ref=part_send.at[0, 0, 0], dst_ref=part_recv.at[me],
            send_sem=part_ssem.at[other], recv_sem=part_rsem.at[me],
            device_id=where, device_id_type=MESH,
        ).wait_send()

    for i in range(1, n_gy):
        tile_copy(stat_a, i, stat_send, stat_recv, p).wait_send()
        tile_copy(stat_b, i, last_send, last_recv, p).wait_send()
    for i in range(1, n_gx):
        x_copy(i, g).wait_send()

    @pl.loop(0, n_gy)
    def _(q):
        for u in range(n_gx):
            out_copy(q, u).wait()

            @pl.when(jnp.logical_and(q <= p, p + 1 < n_gy))
            def _():
                z_copy(q, u, 1, right_send).wait_send()

            @pl.when(jnp.logical_and(q >= p, p >= 1))
            def _():
                z_copy(q, u, -1, left_send).wait_send()


def on_device(shape, inputs, norm_gain, norm_bias, pre_act, grad_act, up_weight):
    n_gx, n_gy, n_gz = shape["gx"], shape["gy"], shape["gz"]
    plane = n_gx * n_gz
    rows_in, width = inputs.shape
    rows = pre_act.shape[0]
    depth = up_weight.shape[1]
    ratio = rows // rows_in
    whole, vmem = pl.BlockSpec(memory_space=pl.ANY), pl.BlockSpec(memory_space=pltpu.VMEM)
    dma = pltpu.SemaphoreType.DMA
    bf16, f32 = jnp.bfloat16, jnp.float32
    slots = n_gx * n_gy
    grad_cols, normed_all, grad_inputs, grad_gain, grad_bias = pl.pallas_call(
        functools.partial(kernel, (n_gx, n_gy, n_gz, rows, rows_in, width, depth)),
        out_shape=(
            jax.ShapeDtypeStruct((n_gx, n_gy, rows, depth), bf16),
            jax.ShapeDtypeStruct((plane, rows_in, width), bf16),
            jax.ShapeDtypeStruct((rows_in, width), bf16),
            jax.ShapeDtypeStruct((width,), f32),
            jax.ShapeDtypeStruct((width,), f32),
        ),
        in_specs=[vmem, vmem, vmem, whole, whole, whole],
        out_specs=(whole, whole, vmem, vmem, vmem),
        scratch_shapes=[
            pltpu.VMEM((n_gx, rows, depth), bf16),
            pltpu.VMEM((n_gx, rows, depth), bf16),
            pltpu.VMEM((n_gx, rows, depth), bf16),
            pltpu.VMEM((depth, width), bf16),
            pltpu.VMEM((n_gy, n_gx, rows, depth), bf16),
            pltpu.VMEM((n_gy, n_gx, ratio, rows_in, width), bf16),
            pltpu.VMEM((plane, rows_in, width), bf16),
            pltpu.VMEM((rows_in, width), f32),
            pltpu.VMEM((rows_in, width), f32),
            pltpu.VMEM((rows_in, width), bf16),
            pltpu.VMEM((plane, 2, width), f32),
            pltpu.VMEM((LANES, LANES), f32),
            pltpu.VMEM((n_gy, SUB, LANES), f32),
            pltpu.VMEM((n_gy, SUB, LANES), f32),
            dma((n_gx,)), dma((n_gx,)), dma, dma((slots,)), dma((slots,)), dma((slots,)), dma((slots,)), dma((n_gx,)),
            dma((n_gy,)), dma((n_gy,)), dma((plane,)), dma((plane,)), dma,
            dma((plane,)), dma((plane,)), dma,
            dma((plane,)), dma((plane,)), dma((n_gy,)), dma((n_gy,)),
        ],
        compiler_params=pltpu.CompilerParams(
            collective_id=0, has_side_effects=True, vmem_limit_bytes=60 * 1024 * 1024
        ),
    )(inputs, norm_gain, norm_bias, pre_act, grad_act, up_weight[0])
    tokens = slots * rows
    weight_block = lax.dot_general(
        grad_cols.reshape(tokens, depth),
        normed_all.reshape(tokens, width),
        (((0,), (0,)), ((), ())),
        preferred_element_type=jnp.float32,
    )
    return grad_inputs, grad_gain, grad_bias, weight_block.reshape(up_weight.shape)


def solution(mesh):
    in_specs = (
        P(("gx", "gz"), "gy"),
        P("gy"),
        P("gy"),
        P(("gx", "gy"), "gz"),
        P(("gx", "gy"), "gz"),
        P("gz", "gx", "gy"),
    )
    out_specs = (P(("gx", "gz"), "gy"), P("gy"), P("gy"), P("gz", "gx", "gy"))
    return jax.shard_map(
        functools.partial(on_device, dict(mesh.shape)),
        mesh=mesh, in_specs=in_specs, out_specs=out_specs, check_vma=False,
    )
```

time: 94.6 us -> 86.5 us (0.914)
  Pallas kernels: 76.8 us -> 72.4 us
  other arithmetic: 3 us -> 0 us
    pallas_call x1, Pallas kernels: 76.8 us -> 72.4 us  [on_device(): pl.pallas_call(functools.partial(kernel, (n_gx, n_gy, n_gz, rows, rows_in...]
    convert_element_type x1 -> x0, other arithmetic: 3 us -> none  [on_device(): grad_local = (grad_act.astype(jnp.float32) * slopes).astype(jnp.bfloat16)]
    broadcast_in_dim x2 -> x0, local copies, waits for them, and re-layouts: 1.2 us -> none  [the longest x1 0.6 us: on_device(): norm_gain[None]]
    unnamed x9, local copies, waits for them, and re-layouts: 0.69 us -> 1.89 us
where the time goes in v3:
time: 86.5 us; the launch traced here: 86.4 us
  Pallas kernels  72.4 us (84%)
  matrix products  11.4 us (13%)
  local copies, waits for them, and re-layouts  1.89 us (2%)
    pallas_call x1, Pallas kernels, on_device(): pl.pallas_call(functools.partial(kernel, (n_gx, n_gy, n_gz, rows, rows_in...  72.4 us
    dot_general x1, matrix products, on_device(): lax.dot_general(grad_cols.reshape(tokens, depth), normed_all.reshape(toke...  11.4 us
    unnamed x9, local copies, waits for them, and re-layouts  1.89 us

profile of v3, /device:TPU:0, one launch (start us, length us, event | category | flops | bytes accessed | tf_op | source)
XLA Modules:
  0.0 86.4 jit_solution(15599330327204922996)
XLA Ops:
  0.6 72.4 %shard_map.93 = (bf16[2,4,64,3072]{3,2,1,0:T(8,128)(2,1)}, bf16[8,64,1536]{2,1,0:T(8,128)(2,1)}, bf16[64,1536]{1,0:T(8,128)(2,1)}, f32[1536]{0:T(1024)}, f32[1536]{0:T(1024)}) custom-call(bf16[64,1536]{1,0:T(8,128)(2,1)} %inputs.1, f32[1536]{0:T(1024)} %gain.1, f32[1536]{0:T(1024)} %bias.1, bf16[64,6144]{1,0:T(8,128)(2,1)} %pre_act.1, ...), custom_call_target="tpu_custom_call" | custom-call | tf_op jit(solution)/shard_map/pallas_call | solution.py:378
  73.0 0.0 copy-start
  73.0 0.0 copy-start.2
  73.0 0.0 copy-start.1
  73.1 11.4 %convolution_bitcast_fusion = f32[1,3072,1536]{2,1,0:T(8,128)} fusion(bf16[512,3072]{1,0:T(8,128)(2,1)} %bitcast.8, bf16[512,1536]{1,0:T(8,128)(2,1)} %bitcast.9), kind=kOutput, calls=%fused_computation | convolution fusion | flops 4831838208 | bytes 23592960 | tf_op jit(solution)/shard_map/dot_general | solution.py:414
  84.5 0.0 copy-done
  84.5 0.7 copy.13
  85.2 0.0 copy-done.2
  85.2 0.6 copy.14
  85.8 0.0 copy-done.1
  85.8 0.6 copy.15
Async XLA Ops:
  73.0 11.5 %copy-start = (bf16[64,1536]{1,0:T(8,128)(2,1)S(1)}, bf16[64,1536]{1,0:T(8,128)(2,1)}, u32[]{:S(2)}) copy-start(bf16[64,1536]{1,0:T(8,128)(2,1)} %get-tuple-element.18) | copy-start | bytes 589828
  73.0 12.2 %copy-start.2 = (f32[1536]{0:T(1024)S(1)}, f32[1536]{0:T(1024)}, u32[]{:S(2)}) copy-start(f32[1536]{0:T(1024)} %get-tuple-element.19) | copy-start | bytes 18436
  73.0 12.7 %copy-start.1 = (f32[1536]{0:T(1024)S(1)}, f32[1536]{0:T(1024)}, u32[]{:S(2)}) copy-start(f32[1536]{0:T(1024)} %get-tuple-element.20) | copy-start | bytes 18436

commit v4 on v3

--- a/solution.py
+++ b/solution.py
@@ -35,13 +35,14 @@
 def kernel(
     sizes,
     inputs, gain, bias, pre_act, grad_act, weight,
-    cols_out, normed_out, grad_inputs, grad_gain, grad_bias,
-    pre_buf, act_buf, stage, w_buf, cols, part_send, part_recv, x_hat, grad_normed, normed_own, sums, pad, stat_a, stat_b,
+    cols_out, normed_out, grad_inputs, grad_sums,
+    pre_buf, act_buf, stage, w_buf, cols, acc, part_send, part_recv, x_hat, grad_normed, normed_own, sums, pad, stat_a, stat_b,
     pre_sem, act_sem, w_sem, out_sem, z_recv, right_send, left_send, x_send,
     stat_send, stat_recv, norm_send, norm_recv, norm_own_sem, part_ssem, part_rsem, part_own_sem,
     sums_send, sums_recv, last_send, last_recv,
 ):
-    n_gx, n_gy, n_gz, rows, rows_in, width, depth = sizes
+    n_gx, n_gy, n_gz, rows, rows_in, width, depth, parts = sizes
+    deep = depth // parts
     ratio = rows // rows_in
     plane = n_gx * n_gz
     g, p, t = lax.axis_index("gx"), lax.axis_index("gy"), lax.axis_index("gz")
@@ -69,31 +70,37 @@
     def _(i):
         pl.semaphore_signal(barrier, inc=1, device_id=plane_peer(i)[1], device_id_type=MESH)
 
-    def half(ref, u):
-        return ref.at[:, pl.ds(pl.multiple_of(u * depth, LANES), depth)]
-
-    loads = []
-    for i in list(range(1, n_gx)) + [0]:
-        u = lax.rem(g + i, n_gx)
-        pair = (
-            pltpu.make_async_copy(half(pre_act, u), pre_buf.at[u], pre_sem.at[u]),
-            pltpu.make_async_copy(half(grad_act, u), act_buf.at[u], act_sem.at[u]),
-        )
-        for copy in pair:
-            copy.start()
-        loads.append((u, pair))
+    def deep_span(h, base=0):
+        return pl.ds(pl.multiple_of(base + h * deep, LANES), deep)
+
+    def load(u, h):
+        source = deep_span(h, u * depth)
+        return (
+            pltpu.make_async_copy(
+                pre_act.at[:, source], pre_buf.at[u, :, deep_span(h)], pre_sem.at[u * parts + h]
+            ),
+            pltpu.make_async_copy(
+                grad_act.at[:, source], act_buf.at[u, :, deep_span(h)], act_sem.at[u * parts + h]
+            ),
+        )
+
+    order = [lax.rem(g + i, n_gx) for i in list(range(1, n_gx)) + [0]]
+    for h in range(parts):
+        for u in order:
+            for copy in load(u, h):
+                copy.start()
     w_copy = pltpu.make_async_copy(weight, w_buf, w_sem)
     w_copy.start()
 
-    step = next(n for n in (384, 256, LANES) if depth % n == 0)
-
-    def gelu_grad(u, pair, out):
-        for copy in pair:
+    step = next(n for n in (384, 256, LANES) if deep % n == 0)
+
+    def gelu_grad(u, h, out):
+        for copy in load(u, h):
             copy.wait()
 
-        @pl.loop(0, depth // step)
+        @pl.loop(0, deep // step)
         def _(c):
-            span = pl.ds(pl.multiple_of(c * step, step), step)
+            span = pl.ds(pl.multiple_of(h * deep + c * step, LANES), step)
             pre = pre_buf[u, :, span].astype(jnp.float32)
             slopes = (
                 0.5 * (1.0 + lax.erf(pre * root_half))
@@ -101,11 +108,6 @@
             )
             out[:, span] = (act_buf[u, :, span].astype(jnp.float32) * slopes).astype(jnp.bfloat16)
 
-    for u, pair in loads[:-1]:
-        gelu_grad(u, pair, stage.at[u])
-
-    pl.semaphore_wait(barrier, n_gy - 1 + plane - 1)
-
     def tile_copy(buf, i, ssem, rsem, source):
         return pltpu.make_async_remote_copy(
             src_ref=buf.at[source], dst_ref=buf.at[source],
@@ -113,40 +115,45 @@
             device_id={"gy": line_peer(i)}, device_id_type=MESH,
         )
 
-    def x_copy(i, source):
+    def x_copy(i, source, h):
         u = lax.rem(g + i, n_gx)
         return pltpu.make_async_remote_copy(
-            src_ref=stage.at[u],
-            dst_ref=cols.at[p, source],
-            send_sem=x_send.at[u], recv_sem=z_recv.at[slot(p, source)],
+            src_ref=stage.at[u, :, deep_span(h)],
+            dst_ref=cols.at[p, source, :, deep_span(h)],
+            send_sem=x_send.at[u], recv_sem=z_recv.at[slot(p, source) * parts + h],
             device_id={"gx": u}, device_id_type=MESH,
         )
 
-    def z_copy(q, u, step, sems):
-        return pltpu.make_async_remote_copy(
-            src_ref=cols.at[q, u], dst_ref=cols.at[q, u],
-            send_sem=sems.at[slot(q, u)], recv_sem=z_recv.at[slot(q, u)],
+    def z_copy(q, u, h, step, sems):
+        return pltpu.make_async_remote_copy(
+            src_ref=cols.at[q, u, :, deep_span(h)], dst_ref=cols.at[q, u, :, deep_span(h)],
+            send_sem=sems.at[slot(q, u)], recv_sem=z_recv.at[slot(q, u) * parts + h],
             device_id={"gy": lax.rem(p + step + n_gy, n_gy)}, device_id_type=MESH,
         )
 
     def out_copy(q, u):
         return pltpu.make_async_copy(cols.at[q, u], cols_out.at[u, q], out_sem.at[slot(q, u)])
 
-    def pass_right(q, u):
+    def pass_right(q, u, h):
         @pl.when(p + 1 < n_gy)
         def _():
-            z_copy(q, u, 1, right_send).start()
-
-    def pass_left(q, u):
+            z_copy(q, u, h, 1, right_send).start()
+
+    def pass_left(q, u, h):
         @pl.when(p >= 1)
         def _():
-            z_copy(q, u, -1, left_send).start()
-
-    for i in range(1, n_gx):
-        x_copy(i, g).start()
-    gelu_grad(loads[-1][0], loads[-1][1], cols.at[p, g])
-    pass_right(p, g)
-    pass_left(p, g)
+            z_copy(q, u, h, -1, left_send).start()
+
+    for h in range(parts):
+        for i in range(1, n_gx):
+            u = lax.rem(g + i, n_gx)
+            gelu_grad(u, h, stage.at[u])
+            if h == 0 and i == 1:
+                pl.semaphore_wait(barrier, n_gy - 1 + plane - 1)
+            x_copy(i, g, h).start()
+        gelu_grad(g, h, cols.at[p, g])
+        pass_right(p, g, h)
+        pass_left(p, g, h)
     out_copy(p, g).start()
 
     widened = inputs[...].astype(jnp.float32)
@@ -159,9 +166,13 @@
 
     for i in range(1, n_gx):
         u = lax.rem(g + i, n_gx)
-        x_copy(i, u).wait_recv()
-        pass_right(p, u)
-        pass_left(p, u)
+
+        @pl.loop(0, parts)
+        def _(h):
+            x_copy(i, u, h).wait_recv()
+            pass_right(p, u, h)
+            pass_left(p, u, h)
+
         out_copy(p, u).start()
     for i in range(1, n_gy):
         tile_copy(stat_a, i, stat_send, stat_recv, line_peer(i)).wait_recv()
@@ -197,56 +208,51 @@
             device_id={"gx": u, "gz": owner}, device_id_type=MESH,
         )
 
-    def multiply(q, units):
-        count = n_gx if units is None else 1
-
+    def send_parts(q, u, span):
+        for j in range(ratio):
+            mine = jnp.logical_and(u == g, q * ratio + j == t)
+
+            @pl.when(mine)
+            def _():
+                pltpu.make_async_copy(
+                    part_send.at[q, u, j, :, span], part_recv.at[me, :, span], part_own_sem
+                ).start()
+
+            @pl.when(jnp.logical_not(mine))
+            def _():
+                part_copy(q, u, j, me, span).start()
+
+    def multiply(q):
         @pl.loop(0, width // SEND)
         def _(c):
-            span = pl.ds(pl.multiple_of(c * SEND, SEND), SEND)
-            block = cols[q].reshape(n_gx * rows, depth) if units is None else cols[q, units]
             for part in range(0, SEND, CHUNK):
                 piece = pl.ds(pl.multiple_of(c * SEND + part, CHUNK), CHUNK)
+                block = cols[q].reshape(n_gx * rows, depth)
                 value = jnp.dot(block, w_buf[:, piece], preferred_element_type=jnp.float32)
-                value = value.astype(jnp.bfloat16).reshape(count, ratio, rows_in, CHUNK)
-                if units is None:
-                    part_send[q, :, :, :, piece] = value
-                else:
-                    part_send[q, units, :, :, piece] = value[0]
-            for u in range(n_gx) if units is None else [units]:
-                for j in range(ratio):
-                    mine = jnp.logical_and(u == g, q * ratio + j == t)
-
-                    @pl.when(mine)
-                    def _():
-                        pltpu.make_async_copy(
-                            part_send.at[q, u, j, :, span], part_recv.at[me, :, span], part_own_sem
-                        ).start()
-
-                    @pl.when(jnp.logical_not(mine))
-                    def _():
-                        part_copy(q, u, j, me, span).start()
-
-    multiply(p, None)
-
-    def take(s, k):
-        u = lax.rem(g + k, n_gx)
-
+                part_send[q, :, :, :, piece] = value.astype(jnp.bfloat16).reshape(
+                    n_gx, ratio, rows_in, CHUNK
+                )
+            for u in range(n_gx):
+                send_parts(q, u, pl.ds(pl.multiple_of(c * SEND, SEND), SEND))
+
+    multiply(p)
+
+    def take(s, u, h):
         @pl.when(p - s >= 0)
         def _():
-            z_copy(p - s, u, 1, right_send).wait_recv()
-            pass_right(p - s, u)
-            out_copy(p - s, u).start()
+            z_copy(p - s, u, h, 1, right_send).wait_recv()
+            pass_right(p - s, u, h)
 
         @pl.when(p + s < n_gy)
         def _():
-            z_copy(p + s, u, -1, left_send).wait_recv()
-            pass_left(p + s, u)
-            out_copy(p + s, u).start()
+            z_copy(p + s, u, h, -1, left_send).wait_recv()
+            pass_left(p + s, u, h)
 
     @pl.loop(1, n_gy - 1)
     def _(s):
-        for k in range(n_gx):
-            take(s, k)
+        @pl.loop(0, n_gx * parts)
+        def _(k):
+            take(s, lax.rem(g + k // parts, n_gx), lax.rem(k, parts))
 
         @pl.loop(0, 2)
         def _(side):
@@ -254,14 +260,46 @@
 
             @pl.when(jnp.logical_and(q >= 0, q < n_gy))
             def _():
-                multiply(q, None)
+                for u in range(n_gx):
+                    out_copy(q, u).start()
+                multiply(q)
 
     @pl.when(jnp.logical_or(p == 0, p == n_gy - 1))
     def _():
+        q = n_gy - 1 - p
+
         @pl.loop(0, n_gx)
         def _(k):
-            take(n_gy - 1, k)
-            multiply(n_gy - 1 - p, lax.rem(g + k, n_gx))
+            u = lax.rem(g + k, n_gx)
+            acc[...] = jnp.zeros_like(acc)
+
+            @pl.loop(0, parts - 1)
+            def _(h):
+                take(n_gy - 1, u, h)
+
+                @pl.loop(0, width // CHUNK)
+                def _(c):
+                    piece = pl.ds(pl.multiple_of(c * CHUNK, CHUNK), CHUNK)
+                    acc[:, piece] += jnp.dot(
+                        cols[q, u, :, deep_span(h)], w_buf[deep_span(h), piece],
+                        preferred_element_type=jnp.float32,
+                    )
+
+            take(n_gy - 1, u, parts - 1)
+            out_copy(q, u).start()
+            last = deep_span(parts - 1)
+
+            @pl.loop(0, width // SEND)
+            def _(c):
+                for part in range(0, SEND, CHUNK):
+                    piece = pl.ds(pl.multiple_of(c * SEND + part, CHUNK), CHUNK)
+                    value = acc[:, piece] + jnp.dot(
+                        cols[q, u, :, last], w_buf[last, piece], preferred_element_type=jnp.float32
+                    )
+                    part_send[q, u, :, :, piece] = value.astype(jnp.bfloat16).reshape(
+                        ratio, rows_in, CHUNK
+                    )
+                send_parts(q, u, pl.ds(pl.multiple_of(c * SEND, SEND), SEND))
 
     pltpu.make_async_copy(part_send.at[0, 0, 0], part_recv.at[me], part_own_sem).wait()
 
@@ -324,11 +362,9 @@
     def _(i):
         sums_copy(i, plane_peer(i)[0]).wait_recv()
 
-    both = lax.fori_loop(
+    grad_sums[...] = lax.fori_loop(
         0, plane, lambda i, acc: acc + sums[i], jnp.zeros((2, width), jnp.float32), unroll=8
     )
-    grad_gain[...] = both[0]
-    grad_bias[...] = both[1]
 
     norm_own.wait()
 
@@ -348,7 +384,19 @@
         tile_copy(stat_a, i, stat_send, stat_recv, p).wait_send()
         tile_copy(stat_b, i, last_send, last_recv, p).wait_send()
     for i in range(1, n_gx):
-        x_copy(i, g).wait_send()
+        u = lax.rem(g + i, n_gx)
+        pltpu.make_async_remote_copy(
+            src_ref=stage.at[u], dst_ref=cols.at[p, g],
+            send_sem=x_send.at[u], recv_sem=z_recv.at[0],
+            device_id={"gx": u}, device_id_type=MESH,
+        ).wait_send()
+
+    def sent(q, u, step, sems):
+        return pltpu.make_async_remote_copy(
+            src_ref=cols.at[q, u], dst_ref=cols.at[q, u],
+            send_sem=sems.at[slot(q, u)], recv_sem=z_recv.at[0],
+            device_id={"gy": lax.rem(p + step + n_gy, n_gy)}, device_id_type=MESH,
+        )
 
     @pl.loop(0, n_gy)
     def _(q):
@@ -357,11 +405,11 @@
 
             @pl.when(jnp.logical_and(q <= p, p + 1 < n_gy))
             def _():
-                z_copy(q, u, 1, right_send).wait_send()
+                sent(q, u, 1, right_send).wait_send()
 
             @pl.when(jnp.logical_and(q >= p, p >= 1))
             def _():
-                z_copy(q, u, -1, left_send).wait_send()
+                sent(q, u, -1, left_send).wait_send()
 
 
 def on_device(shape, inputs, norm_gain, norm_bias, pre_act, grad_act, up_weight):
@@ -370,28 +418,29 @@
     rows_in, width = inputs.shape
     rows = pre_act.shape[0]
     depth = up_weight.shape[1]
-    ratio = rows // rows_in
+    parts = next(n for n in (4, 3, 2, 1) if depth % (n * LANES) == 0)
     whole, vmem = pl.BlockSpec(memory_space=pl.ANY), pl.BlockSpec(memory_space=pltpu.VMEM)
     dma = pltpu.SemaphoreType.DMA
     bf16, f32 = jnp.bfloat16, jnp.float32
+    ratio = rows // rows_in
     slots = n_gx * n_gy
-    grad_cols, normed_all, grad_inputs, grad_gain, grad_bias = pl.pallas_call(
-        functools.partial(kernel, (n_gx, n_gy, n_gz, rows, rows_in, width, depth)),
+    grad_cols, normed_all, grad_inputs, grad_sums = pl.pallas_call(
+        functools.partial(kernel, (n_gx, n_gy, n_gz, rows, rows_in, width, depth, parts)),
         out_shape=(
             jax.ShapeDtypeStruct((n_gx, n_gy, rows, depth), bf16),
             jax.ShapeDtypeStruct((plane, rows_in, width), bf16),
             jax.ShapeDtypeStruct((rows_in, width), bf16),
-            jax.ShapeDtypeStruct((width,), f32),
-            jax.ShapeDtypeStruct((width,), f32),
+            jax.ShapeDtypeStruct((2, width), f32),
         ),
         in_specs=[vmem, vmem, vmem, whole, whole, whole],
-        out_specs=(whole, whole, vmem, vmem, vmem),
+        out_specs=(whole, whole, vmem, vmem),
         scratch_shapes=[
             pltpu.VMEM((n_gx, rows, depth), bf16),
             pltpu.VMEM((n_gx, rows, depth), bf16),
             pltpu.VMEM((n_gx, rows, depth), bf16),
             pltpu.VMEM((depth, width), bf16),
             pltpu.VMEM((n_gy, n_gx, rows, depth), bf16),
+            pltpu.VMEM((rows, width), f32),
             pltpu.VMEM((n_gy, n_gx, ratio, rows_in, width), bf16),
             pltpu.VMEM((plane, rows_in, width), bf16),
             pltpu.VMEM((rows_in, width), f32),
@@ -401,7 +450,7 @@
             pltpu.VMEM((LANES, LANES), f32),
             pltpu.VMEM((n_gy, SUB, LANES), f32),
             pltpu.VMEM((n_gy, SUB, LANES), f32),
-            dma((n_gx,)), dma((n_gx,)), dma, dma((slots,)), dma((slots,)), dma((slots,)), dma((slots,)), dma((n_gx,)),
+            dma((n_gx * parts,)), dma((n_gx * parts,)), dma, dma((slots,)), dma((slots * parts,)), dma((slots,)), dma((slots,)), dma((n_gx,)),
             dma((n_gy,)), dma((n_gy,)), dma((plane,)), dma((plane,)), dma,
             dma((plane,)), dma((plane,)), dma,
             dma((plane,)), dma((plane,)), dma((n_gy,)), dma((n_gy,)),
@@ -417,7 +466,7 @@
         (((0,), (0,)), ((), ())),
         preferred_element_type=jnp.float32,
     )
-    return grad_inputs, grad_gain, grad_bias, weight_block.reshape(up_weight.shape)
+    return grad_inputs, grad_sums[0], grad_sums[1], weight_block.reshape(up_weight.shape)
 
 
 def solution(mesh):

time: 86.5 us -> 84.8 us (0.980)
  Pallas kernels: 72.4 us -> 71.2 us
    unnamed x9 -> x5, local copies, waits for them, and re-layouts: 1.89 us -> 0.69 us
    pallas_call x1, Pallas kernels: 72.4 us -> 71.2 us  [on_device(): pl.pallas_call(functools.partial(kernel, (n_gx, n_gy, n_gz, rows, rows_in...]
where the time goes in v4:
time: 84.8 us; the launch traced here: 84.6 us
  Pallas kernels  71.2 us (84%)
  matrix products  11.4 us (13%)
  local copies, waits for them, and re-layouts  1.31 us (2%)
    pallas_call x1, Pallas kernels, on_device(): pl.pallas_call(functools.partial(kernel, (n_gx, n_gy, n_gz, rows, rows_in...  71.2 us
    dot_general x1, matrix products, on_device(): lax.dot_general(grad_cols.reshape(tokens, depth), normed_all.reshape(toke...  11.4 us

profile of v4, /device:TPU:0, one launch (start us, length us, event | category | flops | bytes accessed | tf_op | source)
XLA Modules:
  0.0 84.6 jit_solution(13294865364544946051)
XLA Ops:
  0.6 71.2 %shard_map.93 = (bf16[2,4,64,3072]{3,2,1,0:T(8,128)(2,1)}, bf16[8,64,1536]{2,1,0:T(8,128)(2,1)}, bf16[64,1536]{1,0:T(8,128)(2,1)}, f32[2,1536]{1,0:T(2,128)}) custom-call(bf16[64,1536]{1,0:T(8,128)(2,1)} %inputs.1, f32[1536]{0:T(1024)} %gain.1, f32[1536]{0:T(1024)} %bias.1, bf16[64,6144]{1,0:T(8,128)(2,1)} %pre_act.1, bf16[64,6144]{1,0:T(8,128)(2,1)} %grad_act.1, ...), custom_call_target="tpu_custom_call" | custom-call | tf_op jit(solution)/shard_map/pallas_call | solution.py:427
  71.9 0.0 copy-start.1
  71.9 0.0 copy-start
  71.9 11.4 %convolution_bitcast_fusion = f32[1,3072,1536]{2,1,0:T(8,128)} fusion(bf16[512,3072]{1,0:T(8,128)(2,1)} %bitcast.8, bf16[512,1536]{1,0:T(8,128)(2,1)} %bitcast.9), kind=kOutput, calls=%fused_computation | convolution fusion | flops 4831838208 | bytes 23592960 | tf_op jit(solution)/shard_map/dot_general | solution.py:463
  83.3 0.0 copy-done.1
  83.3 0.6 slice_reduce_fusion
  84.0 0.0 copy-done
  84.0 0.7 copy.11
Async XLA Ops:
  71.9 11.4 %copy-start.1 = (f32[2,1536]{1,0:T(2,128)S(1)}, f32[2,1536]{1,0:T(2,128)}, u32[]{:S(2)}) copy-start(f32[2,1536]{1,0:T(2,128)} %get-tuple-element.9) | copy-start | bytes 36868
  71.9 12.1 %copy-start = (bf16[64,1536]{1,0:T(8,128)(2,1)S(1)}, bf16[64,1536]{1,0:T(8,128)(2,1)}, u32[]{:S(2)}) copy-start(bf16[64,1536]{1,0:T(8,128)(2,1)} %get-tuple-element.18) | copy-start | bytes 589828

commit v5 on v4

--- a/solution.py
+++ b/solution.py
@@ -410,6 +410,18 @@
             @pl.when(jnp.logical_and(q >= p, p >= 1))
             def _():
                 sent(q, u, -1, left_send).wait_send()
+
+
+def weight_kernel(cols, normed, inputs_in, sums_in, inputs_out, gain_out, bias_out, out):
+    @pl.when(pl.program_id(0) == 0)
+    def _():
+        inputs_out[...] = inputs_in[...]
+        gain_out[...] = sums_in[0]
+        bias_out[...] = sums_in[1]
+
+    out[...] = lax.dot_general(
+        cols[...], normed[...], (((0,), (0,)), ((), ())), preferred_element_type=jnp.float32
+    )
 
 
 def on_device(shape, inputs, norm_gain, norm_bias, pre_act, grad_act, up_weight):
@@ -460,13 +472,33 @@
         ),
     )(inputs, norm_gain, norm_bias, pre_act, grad_act, up_weight[0])
     tokens = slots * rows
-    weight_block = lax.dot_general(
-        grad_cols.reshape(tokens, depth),
-        normed_all.reshape(tokens, width),
-        (((0,), (0,)), ((), ())),
-        preferred_element_type=jnp.float32,
-    )
-    return grad_inputs, grad_sums[0], grad_sums[1], weight_block.reshape(up_weight.shape)
+    tile = next(n for n in (512, 384, 256, LANES) if depth % n == 0)
+    fixed = lambda *shape: pl.BlockSpec(shape, lambda i: (0,) * len(shape))
+    return pl.pallas_call(
+        weight_kernel,
+        grid=(depth // tile,),
+        out_shape=(
+            jax.ShapeDtypeStruct((rows_in, width), bf16),
+            jax.ShapeDtypeStruct((width,), f32),
+            jax.ShapeDtypeStruct((width,), f32),
+            jax.ShapeDtypeStruct((1, depth, width), f32),
+        ),
+        in_specs=[
+            pl.BlockSpec((tokens, tile), lambda i: (0, i)),
+            fixed(tokens, width), fixed(rows_in, width), fixed(2, width),
+        ],
+        out_specs=(
+            fixed(rows_in, width), fixed(width), fixed(width),
+            pl.BlockSpec((None, tile, width), lambda i: (0, i, 0)),
+        ),
+        compiler_params=pltpu.CompilerParams(
+            dimension_semantics=("arbitrary",), vmem_limit_bytes=48 * 1024 * 1024
+        ),
+        cost_estimate=pl.CostEstimate(
+            flops=2 * tokens * depth * width, transcendentals=0,
+            bytes_accessed=2 * tokens * (depth + width) + 4 * depth * width,
+        ),
+    )(grad_cols.reshape(tokens, depth), normed_all.reshape(tokens, width), grad_inputs, grad_sums)
 
 
 def solution(mesh):

time: 84.8 us -> 86.3 us (1.018)
  matrix products: 11.4 us -> 0 us
  Pallas kernels: 71.2 us -> 80.5 us
  local copies, waits for them, and re-layouts: 1.31 us -> 4.92 us
    dot_general x1 -> x0, matrix products: 11.4 us -> none  [on_device(): lax.dot_general(grad_cols.reshape(tokens, depth), normed_all.reshape(toke...]
    pallas_call x0 -> x1, Pallas kernels: none -> 9.23 us  [on_device(): pl.pallas_call(weight_kernel, grid=(depth // tile,), out_shape=(jax.Shape...]
    unnamed x5 -> x8, local copies, waits for them, and re-layouts: 0.69 us -> 4.92 us
where the time goes in v5:
time: 86.3 us; the launch traced here: 86.1 us
  Pallas kernels  80.5 us (93%)
  local copies, waits for them, and re-layouts  4.92 us (6%)
    pallas_call x1, Pallas kernels, on_device(): pl.pallas_call(functools.partial(kernel, (n_gx, n_gy, n_gz, rows, rows_in...  71.3 us
    pallas_call x1, Pallas kernels, on_device(): pl.pallas_call(weight_kernel, grid=(depth // tile,), out_shape=(jax.Shape...  9.23 us
    unnamed x8, local copies, waits for them, and re-layouts  4.92 us

profile of v5, /device:TPU:0, one launch (start us, length us, event | category | flops | bytes accessed | tf_op | source)
XLA Modules:
  0.0 86.1 jit_solution(2638341556765958274)
XLA Ops:
  0.6 71.3 %shard_map.93 = (bf16[2,4,64,3072]{3,2,1,0:T(8,128)(2,1)}, bf16[8,64,1536]{2,1,0:T(8,128)(2,1)}, bf16[64,1536]{1,0:T(8,128)(2,1)}, f32[2,1536]{1,0:T(2,128)}) custom-call(bf16[64,1536]{1,0:T(8,128)(2,1)} %inputs.1, f32[1536]{0:T(1024)} %gain.1, f32[1536]{0:T(1024)} %bias.1, bf16[64,6144]{1,0:T(8,128)(2,1)} %pre_act.1, bf16[64,6144]{1,0:T(8,128)(2,1)} %grad_act.1, ...), custom_call_target="tpu_custom_call" | custom-call | tf_op jit(solution)/shard_map/pallas_call | solution.py:439
  71.9 0.0 copy-start
  71.9 1.9 %copy-done = bf16[2,4,64,3072]{3,2,1,0:T(8,128)(2,1)S(1)} copy-done((bf16[2,4,64,3072]{3,2,1,0:T(8,128)(2,1)S(1)}, bf16[2,4,64,3072]{3,2,1,0:T(8,128)(2,1)}, u32[]{:S(2)}) %copy-start) | copy-done | bytes 3145752
  73.8 0.0 copy-start.1
  73.8 1.4 %copy-done.1 = bf16[8,64,1536]{2,1,0:T(8,128)(2,1)S(1)} copy-done((bf16[8,64,1536]{2,1,0:T(8,128)(2,1)S(1)}, bf16[8,64,1536]{2,1,0:T(8,128)(2,1)}, u32[]{:S(2)}) %copy-start.1) | copy-done | bytes 1572888
  75.2 0.0 copy-start.2
  75.2 0.9 %copy-done.2 = bf16[64,1536]{1,0:T(8,128)(2,1)S(1)} copy-done((bf16[64,1536]{1,0:T(8,128)(2,1)S(1)}, bf16[64,1536]{1,0:T(8,128)(2,1)}, u32[]{:S(2)}) %copy-start.2) | copy-done | bytes 196632
  76.1 0.0 copy-start.3
  76.1 0.7 copy-done.3
  76.8 9.2 %shard_map.94 = (bf16[64,1536]{1,0:T(8,128)(2,1)}, f32[1536]{0:T(1024)}, f32[1536]{0:T(1024)}, f32[1,3072,1536]{2,1,0:T(8,128)}) custom-call(bf16[512,3072]{1,0:T(8,128)(2,1)S(1)} %bitcast.3, bf16[512,1536]{1,0:T(8,128)(2,1)S(1)} %bitcast.4, bf16[64,1536]{1,0:T(8,128)(2,1)S(1)} %copy-done.2, f32[2,1536]{1,0:T(2,128)S(1)} %copy-done.3), custom_call_target="tpu_custom_call" | custom-call | flops 4831838208 | bytes 23592960 | tf_op jit(solution)/shard_map/pallas_call | solution.py:477
Async XLA Ops:
  71.9 1.9 %copy-start = (bf16[2,4,64,3072]{3,2,1,0:T(8,128)(2,1)S(1)}, bf16[2,4,64,3072]{3,2,1,0:T(8,128)(2,1)}, u32[]{:S(2)}) copy-start(bf16[2,4,64,3072]{3,2,1,0:T(8,128)(2,1)} %get-tuple-element.8) | copy-start | bytes 9437188
  73.8 1.4 %copy-start.1 = (bf16[8,64,1536]{2,1,0:T(8,128)(2,1)S(1)}, bf16[8,64,1536]{2,1,0:T(8,128)(2,1)}, u32[]{:S(2)}) copy-start(bf16[8,64,1536]{2,1,0:T(8,128)(2,1)} %get-tuple-element.9) | copy-start | bytes 4718596
  75.2 0.9 %copy-start.2 = (bf16[64,1536]{1,0:T(8,128)(2,1)S(1)}, bf16[64,1536]{1,0:T(8,128)(2,1)}, u32[]{:S(2)}) copy-start(bf16[64,1536]{1,0:T(8,128)(2,1)} %get-tuple-element.10.inputs_in) | copy-start | bytes 589828
  76.1 0.7 copy-start.3

commit v6 on v5

--- a/solution.py
+++ b/solution.py
@@ -492,7 +492,7 @@
             pl.BlockSpec((None, tile, width), lambda i: (0, i, 0)),
         ),
         compiler_params=pltpu.CompilerParams(
-            dimension_semantics=("arbitrary",), vmem_limit_bytes=48 * 1024 * 1024
+            dimension_semantics=("arbitrary",), vmem_limit_bytes=67_043_328
         ),
         cost_estimate=pl.CostEstimate(
             flops=2 * tokens * depth * width, transcendentals=0,

time: 86.3 us -> 83.2 us (0.964)
  local copies, waits for them, and re-layouts: 4.92 us -> 0 us
  Pallas kernels: 80.5 us -> 82.4 us
    unnamed x8 -> x0, local copies, waits for them, and re-layouts: 4.92 us -> none
    pallas_call x1, Pallas kernels: 9.23 us -> 11.1 us  [on_device(): pl.pallas_call(weight_kernel, grid=(depth // tile,), out_shape=(jax.Shape...]
where the time goes in v6:
time: 83.2 us; the launch traced here: 83 us
  Pallas kernels  82.4 us (99%)
    pallas_call x1, Pallas kernels, on_device(): pl.pallas_call(functools.partial(kernel, (n_gx, n_gy, n_gz, rows, rows_in...  71.3 us
    pallas_call x1, Pallas kernels, on_device(): pl.pallas_call(weight_kernel, grid=(depth // tile,), out_shape=(jax.Shape...  11.1 us

profile of v6, /device:TPU:0, one launch (start us, length us, event | category | flops | bytes accessed | tf_op | source)
XLA Modules:
  0.0 83.0 jit_solution(5859143192444399430)
XLA Ops:
  0.6 71.3 %shard_map.93 = (bf16[2,4,64,3072]{3,2,1,0:T(8,128)(2,1)}, bf16[8,64,1536]{2,1,0:T(8,128)(2,1)}, bf16[64,1536]{1,0:T(8,128)(2,1)}, f32[2,1536]{1,0:T(2,128)}) custom-call(bf16[64,1536]{1,0:T(8,128)(2,1)} %inputs.1, f32[1536]{0:T(1024)} %gain.1, f32[1536]{0:T(1024)} %bias.1, bf16[64,6144]{1,0:T(8,128)(2,1)} %pre_act.1, bf16[64,6144]{1,0:T(8,128)(2,1)} %grad_act.1, ...), custom_call_target="tpu_custom_call" | custom-call | tf_op jit(solution)/shard_map/pallas_call | solution.py:439
  71.9 11.1 %shard_map.94 = (bf16[64,1536]{1,0:T(8,128)(2,1)}, f32[1536]{0:T(1024)}, f32[1536]{0:T(1024)}, f32[1,3072,1536]{2,1,0:T(8,128)}) custom-call(bf16[512,3072]{1,0:T(8,128)(2,1)} %bitcast.4, bf16[512,1536]{1,0:T(8,128)(2,1)} %bitcast.5, bf16[64,1536]{1,0:T(8,128)(2,1)} %get-tuple-element.10.inputs_in, f32[2,1536]{1,0:T(2,128)} %get-tuple-element.11.sums_in), custom_call_target="tpu_custom_call" | custom-call | flops 4831838208 | bytes 23592960 | tf_op jit(solution)/shard_map/pallas_call | solution.py:477
